TPU v7x, 32 devices: a whole 2x2x4 slice. The times are simulated.
32 devices in a mesh: dp: 16 (over z, y, x), tensor: 2 (over core).
Axes of the slice: x: 2, y: 2, z: 4, core: 2. Of those that a mesh axis runs over, the one named last changes fastest.
Arguments:
- tokens: bfloat16 [32, 1024, 768], P('dp'), may hold values from -6 to 6
- segments: int32 [32, 1024], P('dp'), may hold values from 0 to 8, as said below
- qkv_weight: bfloat16 [768, 3, 768], P(('dp', 'tensor')), may hold values from -0.21875 to 0.21875
- out_weight: bfloat16 [768, 768], P(('dp', 'tensor')), may hold values from -1.75 to 1.75
- norm_gain: bfloat16 [768, 2], P(('dp', 'tensor')), may hold values from 0.5 to 1.5
- norm_shift: bfloat16 [768, 2], P(('dp', 'tensor')), may hold values from -3 to 3
- gate_up: bfloat16 [768, 2, 3072], P('dp', None, 'tensor'), may hold values from -0.21875 to 0.21875
- down_weight: bfloat16 [768, 3072], P('dp', 'tensor'), may hold values from -0.109375 to 0.109375
- cotangent: bfloat16 [32, 1024, 768], P('dp', 'tensor'), may hold values from -6 to 6
Outputs:
- output: bfloat16 [32, 1024, 768], P('dp', 'tensor')
- input_grad: float32 [32, 1024, 768], P('dp', 'tensor')
- qkv_grad: float32 [768, 3, 768], P(('dp', 'tensor'))
- out_weight_grad: float32 [768, 768], P(('dp', 'tensor'))
- gain_grad: float32 [768, 2], P(('dp', 'tensor'))
- shift_grad: float32 [768, 2], P(('dp', 'tensor'))
- gate_up_grad: float32 [768, 2, 3072], P('dp', None, 'tensor')
- down_grad: float32 [768, 3072], P('dp', 'tensor')
Inputs may be any that keep to these rules, and one draw needn't show every extreme that they name: `segments`: never falling along a sequence; each of the 8 documents has at least one token, and exactly one of them holds 512 tokens, more than any other; the value 8 marks padding, which every sequence has.
All inputs are finite; a program needn't handle non-finite values.
Results may differ from a plain program's by a relative error of at most 0.015.
Values may be sent and summed in bfloat16 or wider, within the bound.
No kernel may reach another device: no remote copies, remote signals or barrier semaphores. Data moves between devices by JAX's collectives and lax.ppermute only.
A program may use at most 320 MiB of HBM per device.

v0:
```python
import jax
import jax.numpy as jnp
from jax import lax
from jax.sharding import PartitionSpec as P

D = 768
HEADS = 12
HEAD = 64
SEQ = 1024
NDOC = 8


EPSILON = 1e-05
MASKED = -1e30


def for_sending(value):
    return jax.tree.map(lambda a: a.astype(jnp.bfloat16) if a.dtype == jnp.float32 else a, value)


def rotary_tables(segment_row):
    labels = jnp.arange(NDOC + 1, dtype=jnp.int32)
    member = (segment_row[:, None] == labels[None, :]).astype(jnp.int32)
    counts = jnp.sum(member, axis=0)
    starts = jnp.concatenate([jnp.zeros((1,), jnp.int32), jnp.cumsum(counts)[:-1]])
    offset = jnp.sum(member * starts[None, :], axis=1)
    position = (jnp.arange(SEQ, dtype=jnp.int32) - offset).astype(jnp.float32)
    exponent = -2.0 * jnp.arange(HEAD // 2).astype(jnp.float32) / HEAD
    frequency = jnp.power(jnp.float32(1000.0), exponent)
    angle = position[:, None] * frequency[None, :]
    return (jnp.cos(angle)[:, None, :], jnp.sin(angle)[:, None, :])


def rotate(vector, cosine, sine):
    half = vector.shape[-1] // 2
    first_half = vector[..., :half]
    second_half = vector[..., half:]
    return jnp.concatenate(
        [first_half * cosine - second_half * sine, second_half * cosine + first_half * sine],
        axis=-1,
    )


def unrotate(gradient, cosine, sine):

    def turned(vector):
        return rotate(vector, cosine, sine)

    _, pullback = jax.vjp(turned, gradient)
    return pullback(gradient)[0]


def layer_norm(vector, gain, shift):
    center = vector - jnp.mean(vector, axis=-1, keepdims=True)
    variance = jnp.mean(center * center, axis=-1, keepdims=True)
    return center * lax.rsqrt(variance + EPSILON) * gain + shift


def swiglu_piece(gate, upper):
    return jax.nn.silu(gate) * upper


def accumulate(total, term):
    if total is None:
        return term
    return tuple((left + right for left, right in zip(total, term)))


def per_device(
    tokens, segments, qkv_weight, out_weight, norm_gain, norm_shift, gate_up, down_weight, cotangent
):
    tensor_size = lax.axis_size("tensor")
    own_rows = SEQ // tensor_size
    row_start = lax.axis_index("tensor") * own_rows
    score_scale = HEAD ** (-0.5)
    qkv_full, out_full, gain_full, shift_full = (
        lax.all_gather(qkv_weight, ("dp", "tensor"), axis=0, tiled=True),
        lax.all_gather(out_weight, ("dp", "tensor"), axis=0, tiled=True),
        lax.all_gather(norm_gain, ("dp", "tensor"), axis=0, tiled=True),
        lax.all_gather(norm_shift, ("dp", "tensor"), axis=0, tiled=True),
    )
    gains = gain_full.astype(jnp.float32)
    shifts = shift_full.astype(jnp.float32)
    gate_up_full, down_full = (
        lax.all_gather(gate_up, "dp", axis=0, tiled=True),
        lax.all_gather(down_weight, "dp", axis=0, tiled=True),
    )
    batches = tokens.shape[0]
    outputs = []
    input_grads = []
    attn_total = None
    mlp_total = None
    for batch_index in range(batches):
        source = tokens[batch_index]
        own_source = lax.dynamic_slice_in_dim(source, row_start, own_rows, 0)
        segment_row = segments[batch_index]
        cosine, sine = rotary_tables(segment_row)
        own_cos = lax.dynamic_slice_in_dim(cosine, row_start, own_rows, 0)
        own_sin = lax.dynamic_slice_in_dim(sine, row_start, own_rows, 0)
        query_proj = jnp.einsum(
            "sd,de->se", own_source, qkv_full[:, 0], preferred_element_type=jnp.float32
        )
        pair_proj = jnp.einsum(
            "sd,dke->ske", source, qkv_full[:, 1:], preferred_element_type=jnp.float32
        )
        keys = rotate(pair_proj[:, 0].reshape(SEQ, HEADS, HEAD), cosine, sine).astype(jnp.bfloat16)
        values = pair_proj[:, 1].reshape(SEQ, HEADS, HEAD).astype(jnp.bfloat16)
        queries = rotate(query_proj.reshape(own_rows, HEADS, HEAD), own_cos, own_sin).astype(
            jnp.bfloat16
        )
        own_segments = lax.dynamic_slice_in_dim(segment_row, row_start, own_rows, 0)
        allowed = (own_segments[:, None] == segment_row[None, :])[None]
        raw_scores = (
            jnp.einsum("qhe,khe->hqk", queries, keys, preferred_element_type=jnp.float32)
            * score_scale
        )
        masked = jnp.where(allowed, raw_scores, MASKED)
        top_score = jnp.max(masked, axis=-1, keepdims=True)
        logsum = top_score + jnp.log(jnp.sum(jnp.exp(masked - top_score), axis=-1, keepdims=True))
        probs_low = jnp.exp(masked - logsum).astype(jnp.bfloat16)
        context = (
            jnp.einsum("hqk,khe->qhe", probs_low, values, preferred_element_type=jnp.float32)
            .reshape(own_rows, D)
            .astype(jnp.bfloat16)
        )
        attended = jnp.dot(context, out_full, preferred_element_type=jnp.float32)
        hidden_in = own_source.astype(jnp.float32) + attended
        normed = layer_norm(hidden_in, gains[:, 0], shifts[:, 0])
        normed_all = lax.all_gather(normed.astype(jnp.bfloat16), "tensor", axis=0, tiled=True)
        gate_pair = jnp.einsum(
            "sd,dkf->skf", normed_all, gate_up_full, preferred_element_type=jnp.float32
        )
        swiglu = swiglu_piece(gate_pair[:, 0], gate_pair[:, 1]).astype(jnp.bfloat16)
        mlp_out = lax.psum_scatter(
            jnp.einsum("sf,df->sd", swiglu, down_full, preferred_element_type=jnp.float32).astype(
                jnp.bfloat16
            ),
            "tensor",
            scatter_dimension=0,
            tiled=True,
        ).astype(jnp.float32)
        resid = normed + mlp_out
        outputs.append(layer_norm(resid, gains[:, 1], shifts[:, 1]).astype(jnp.bfloat16))
        upstream = cotangent[batch_index].astype(jnp.float32)
        _, second_pull = jax.vjp(layer_norm, resid, gains[:, 1], shifts[:, 1])
        resid_grad, gain_two, shift_two = second_pull(upstream)
        mlp_grad = lax.all_gather(resid_grad.astype(jnp.bfloat16), "tensor", axis=0, tiled=True)
        swiglu_grad = jnp.einsum(
            "sd,df->sf", mlp_grad, down_full, preferred_element_type=jnp.float32
        )
        _, glu_pull = jax.vjp(swiglu_piece, gate_pair[:, 0], gate_pair[:, 1])
        gate_grad, upper_grad = glu_pull(swiglu_grad)
        pair_grad = jnp.stack([gate_grad, upper_grad], axis=1).astype(jnp.bfloat16)
        down_term = jnp.einsum("sd,sf->df", mlp_grad, swiglu, preferred_element_type=jnp.float32)
        gate_up_term = jnp.einsum(
            "sd,skf->dkf", normed_all, pair_grad, preferred_element_type=jnp.float32
        )
        normed_grad = resid_grad + lax.psum_scatter(
            jnp.einsum("skf,dkf->sd", pair_grad, gate_up_full, preferred_element_type=jnp.float32),
            "tensor",
            scatter_dimension=0,
            tiled=True,
        )
        _, first_pull = jax.vjp(layer_norm, hidden_in, gains[:, 0], shifts[:, 0])
        hidden_grad, gain_one, shift_one = first_pull(normed_grad)
        attended_grad = hidden_grad.astype(jnp.bfloat16)
        out_term = jnp.einsum(
            "sd,se->de", context, attended_grad, preferred_element_type=jnp.float32
        )
        context_grad = (
            jnp.einsum("se,de->sd", attended_grad, out_full, preferred_element_type=jnp.float32)
            .astype(jnp.bfloat16)
            .reshape(own_rows, HEADS, HEAD)
        )
        probs = jnp.exp(masked - logsum)
        weights_grad = jnp.einsum(
            "qhe,khe->hqk", context_grad, values, preferred_element_type=jnp.float32
        )
        row_delta = jnp.sum(probs * weights_grad, axis=-1, keepdims=True)
        score_grad = (probs * (weights_grad - row_delta)).astype(jnp.bfloat16)
        query_grad = (
            jnp.einsum("hqk,khe->qhe", score_grad, keys, preferred_element_type=jnp.float32)
            * score_scale
        )
        key_part = (
            jnp.einsum("hqk,qhe->khe", score_grad, queries, preferred_element_type=jnp.float32)
            * score_scale
        )
        value_part = jnp.einsum(
            "hqk,qhe->khe", probs_low, context_grad, preferred_element_type=jnp.float32
        )
        key_value = lax.psum_scatter(
            jnp.stack(
                [
                    key_part.reshape(lax.axis_size("tensor") * own_rows, D),
                    value_part.reshape(lax.axis_size("tensor") * own_rows, D),
                ],
                axis=1,
            ).astype(jnp.bfloat16),
            "tensor",
            scatter_dimension=0,
            tiled=True,
        ).astype(jnp.float32)
        query_back = unrotate(query_grad, own_cos, own_sin).reshape(own_rows, D)
        key_back = unrotate(
            key_value[:, 0].reshape(own_rows, HEADS, HEAD), own_cos, own_sin
        ).reshape(own_rows, D)
        proj_grad = jnp.stack([query_back, key_back, key_value[:, 1]], axis=1).astype(jnp.bfloat16)
        input_grads.append(
            hidden_grad
            + jnp.einsum("ske,dke->sd", proj_grad, qkv_full, preferred_element_type=jnp.float32)
        )
        qkv_term = jnp.einsum(
            "sd,ske->dke", own_source, proj_grad, preferred_element_type=jnp.float32
        )
        gain_term = jnp.stack([gain_one, gain_two], axis=1)
        shift_term = jnp.stack([shift_one, shift_two], axis=1)
        attn_terms = (qkv_term, out_term, gain_term, shift_term)
        mlp_terms = (gate_up_term, down_term)
        attn_total = accumulate(attn_total, attn_terms)
        mlp_total = accumulate(mlp_total, mlp_terms)
    attn_final = lax.psum_scatter(attn_total, ("dp", "tensor"), scatter_dimension=0, tiled=True)
    mlp_final = jax.tree.map(
        lambda part: part.astype(jnp.float32),
        lax.psum_scatter(for_sending(mlp_total), "dp", scatter_dimension=0, tiled=True),
    )
    return (
        jnp.stack(outputs, axis=0),
        jnp.stack(input_grads, axis=0),
        attn_final[0],
        attn_final[1],
        attn_final[2],
        attn_final[3],
        mlp_final[0],
        mlp_final[1],
    )


def solution(mesh):
    in_specs = (
        P("dp", None, None),
        P("dp", None),
        P(("dp", "tensor"), None, None),
        P(("dp", "tensor"), None),
        P(("dp", "tensor"), None),
        P(("dp", "tensor"), None),
        P("dp", None, "tensor"),
        P("dp", "tensor"),
        P("dp", "tensor", None),
    )
    out_specs = (
        P("dp", "tensor", None),
        P("dp", "tensor", None),
        P(("dp", "tensor"), None, None),
        P(("dp", "tensor"), None),
        P(("dp", "tensor"), None),
        P(("dp", "tensor"), None),
        P("dp", None, "tensor"),
        P("dp", "tensor"),
    )
    return jax.shard_map(
        per_device, mesh=mesh, in_specs=in_specs, out_specs=out_specs, check_vma=False
    )
```

profile of v0, /device:TPU:0, one launch (start us, length us, event | category | flops | bytes accessed | tf_op | source)
XLA Modules:
  0.0 1118.4 jit_solution(12078106832621006641)
XLA Ops:
  17.0 43.1 %all-gather = bf16[32,24,2]{1,2,0:T(2,128)(2,1)S(1)} all-gather(bf16[1,24,2]{1,2,0:T(2,128)(2,1)S(1)} %bitcast.273), channel_id=1, replica_groups=mesh['dp'=16,'tensor'=2] {'dp','tensor'}, dimensions={0}, use_global_device_ids=true | all-gather | bytes 3168 | tf_op jit(solution)/shard_map/all_gather | solution.py:79
  60.4 36.7 %all-gather.1 = bf16[32,24,2]{1,2,0:T(2,128)(2,1)S(1)} all-gather(bf16[1,24,2]{1,2,0:T(2,128)(2,1)S(1)} %bitcast.274), channel_id=1, replica_groups=mesh['dp'=16,'tensor'=2] {'dp','tensor'}, dimensions={0}, use_global_device_ids=true | all-gather | bytes 3168 | tf_op jit(solution)/shard_map/all_gather | solution.py:80
  109.1 10.7 fusion
  119.8 11.8 %exponential_reduce_fusion.1 = f32[12,512]{1,0:T(8,128)S(1)} fusion(f32[12,512,1024]{2,1,0:T(8,128)} %get-tuple-element.133, f32[12,512]{1,0:T(8,128)S(1)} %get-tuple-element.132, pred[512,1024]{1,0:T(8,128)(4,1)S(1)} %broadcast_compare_fusion.1), kind=kLoop, calls=%fused_computation.8 | loop fusion | flops 25159680 | bytes 25739264 | tf_op jit(solution)/shard_map/reduce_sum | solution.py:119
  133.1 12.4 %convolution_convert_fusion.7 = bf16[12,64,512]{2,1,0:T(8,128)(2,1)} fusion(bf16[1024,12,64]{0,2,1:T(8,128)(2,1)S(1)} %bitcast.243, f32[12,512,1024]{2,1,0:T(8,128)} %get-tuple-element.133, f32[12,512]{1,0:T(8,128)S(1)} %log_add_fusion.1, pred[512,1024]{1,0:T(8,128)(4,1)S(1)} %broadcast_compare_fusion.1), kind=kOutput, calls=%fused_computation.136 | convolution fusion | flops 830865408 | bytes 28073984 | tf_op jit(solution)/shard_map/hqk,khe->qhe/dot_general | solution.py:122
  164.1 10.8 fusion.1
  174.9 67.0 %all-gather.17.cloned.1.call-done = bf16[768,2,1536]{2,0,1:T(8,128)(2,1)} async-done(((bf16[48,2,1536]{2,0,1:T(8,128)(2,1)}), bf16[768,2,1536]{2,0,1:T(8,128)(2,1)}) %all-gather.17.cloned.1.call-update) | async-done | bytes 4718608 | tf_op jit(solution)/shard_map/all_gather | solution.py:85
  256.7 48.7 %all-gather.19.cloned.1.call-done = bf16[768,1536]{1,0:T(8,128)(2,1)} async-done(((bf16[48,1536]{1,0:T(8,128)(2,1)}), bf16[768,1536]{1,0:T(8,128)(2,1)}) %all-gather.19.cloned.1.call-update) | async-done | bytes 2359312 | tf_op jit(solution)/shard_map/all_gather | solution.py:86
  311.9 12.4 %exponential_reduce_fusion = f32[12,512]{1,0:T(8,128)S(1)} fusion(f32[12,512,1024]{2,1,0:T(8,128)} %get-tuple-element.137, f32[12,512]{1,0:T(8,128)S(1)} %get-tuple-element.136, pred[512,1024]{1,0:T(8,128)(4,1)S(1)} %broadcast_compare_fusion), kind=kLoop, calls=%fused_computation.5 | loop fusion | flops 25159680 | bytes 25739264 | tf_op jit(solution)/shard_map/reduce_sum | solution.py:119
  326.5 11.7 %convolution_convert_fusion.6 = bf16[12,64,512]{2,1,0:T(8,128)(2,1)S(1)} fusion(bf16[1024,12,64]{0,2,1:T(8,128)(2,1)S(1)} %bitcast.245, f32[12,512,1024]{2,1,0:T(8,128)} %get-tuple-element.137, f32[12,512]{1,0:T(8,128)S(1)} %log_add_fusion, pred[512,1024]{1,0:T(8,128)(4,1)S(1)} %broadcast_compare_fusion), kind=kOutput, calls=%fused_computation.135 | convolution fusion | flops 830865408 | bytes 28073984 | tf_op jit(solution)/shard_map/hqk,khe->qhe/dot_general | solution.py:122
  342.9 8.7 all-gather.21.cloned.1.call-done
  371.3 8.6 reduce-scatter.15.cloned.1.call-done
  391.8 8.6 all-gather.25.cloned.1.call-done
  400.3 8.8 fusion.17
  412.0 9.1 fusion.28
  421.2 8.9 fusion.18
  432.7 9.1 fusion.27
  442.0 12.1 %reduce-scatter.17.cloned.1.call-done = f32[512,768]{1,0:T(8,128)} async-done(((f32[1024,768]{1,0:T(8,128)}), f32[512,768]{1,0:T(8,128)}) %reduce-scatter.17.cloned.1.call-update) | async-done | bytes 1572880 | tf_op jit(solution)/shard_map/reduce_scatter | solution.py:158
  465.3 21.4 %multiply_reduce_fusion.1 = (f32[12,512]{1,0:T(8,128)S(1)}, f32[12,512,1024]{2,1,0:T(8,128)}) fusion(f32[12,512,1024]{2,1,0:T(8,128)} %get-tuple-element.133, f32[12,512]{1,0:T(8,128)S(1)} %copy-done.74, pred[512,1024]{1,0:T(8,128)(4,1)S(1)} %copy-done.11, bf16[512,12,64]{0,2,1:T(8,128)(2,1)S(1)} %bitcast.255, bf16[1024,12,64]{0,2,1:T(8,128)(2,1)S(1)} %bitcast.244), kind=kOutput, calls=%fused_computation.3 | convolution fusion | flops 836757504 | bytes 53264384 | tf_op jit(solution)/shard_map/qhe,khe->hqk/dot_general | solution.py:176
  486.7 12.9 %convolution_convert_fusion.1 = bf16[12,64,1024]{2,1,0:T(8,128)(2,1)} fusion(bf16[512,12,64]{0,2,1:T(8,128)(2,1)S(1)} %bitcast.256, f32[12,512,1024]{2,1,0:T(8,128)} %get-tuple-element.133, f32[12,512]{1,0:T(8,128)S(1)} %copy-done.74, pred[512,1024]{1,0:T(8,128)(4,1)S(1)} %copy-done.11), kind=kOutput, calls=%fused_computation.79 | convolution fusion | flops 831258624 | bytes 28073984 | tf_op jit(solution)/shard_map/hqk,qhe->khe/dot_general | solution.py:189
  499.5 17.1 %multiply_convert_fusion.1 = bf16[12,512,1024]{2,1,0:T(8,128)(2,1)S(1)} fusion(f32[12,512,1024]{2,1,0:T(8,128)} %get-tuple-element.143, f32[12,512,1024]{2,1,0:T(8,128)} %get-tuple-element.133, f32[12,512]{1,0:T(8,128)S(1)} %get-tuple-element.142, f32[12,512]{1,0:T(8,128)S(1)} %copy-done.74, pred[512,1024]{1,0:T(8,128)(4,1)S(1)} %copy-done.11), kind=kLoop, calls=%fused_computation.2 | loop fusion | flops 37748736 | bytes 63488000 | tf_op jit(solution)/shard_map/convert_element_type | solution.py:180
  530.7 22.4 %multiply_reduce_fusion = (f32[12,512]{1,0:T(8,128)S(1)}, f32[12,512,1024]{2,1,0:T(8,128)}) fusion(f32[12,512,1024]{2,1,0:T(8,128)} %get-tuple-element.137, f32[12,512]{1,0:T(8,128)S(1)} %log_add_fusion, pred[512,1024]{1,0:T(8,128)(4,1)S(1)} %copy-done.13, bf16[512,12,64]{0,2,1:T(8,128)(2,1)S(1)} %bitcast.253, bf16[1024,12,64]{0,2,1:T(8,128)(2,1)S(1)} %bitcast.246), kind=kOutput, calls=%fused_computation.1 | convolution fusion | flops 836757504 | bytes 53264384 | tf_op jit(solution)/shard_map/qhe,khe->hqk/dot_general | solution.py:176
  553.1 17.1 %multiply_convert_fusion = bf16[12,512,1024]{2,1,0:T(8,128)(2,1)S(1)} fusion(f32[12,512,1024]{2,1,0:T(8,128)} %get-tuple-element.141, f32[12,512,1024]{2,1,0:T(8,128)} %get-tuple-element.137, f32[12,512]{1,0:T(8,128)S(1)} %get-tuple-element.140, f32[12,512]{1,0:T(8,128)S(1)} %log_add_fusion, pred[512,1024]{1,0:T(8,128)(4,1)S(1)} %copy-done.13), kind=kLoop, calls=%fused_computation | loop fusion | flops 37748736 | bytes 63488000 | tf_op jit(solution)/shard_map/convert_element_type | solution.py:180
  576.4 12.8 %convolution_convert_fusion = bf16[12,64,1024]{2,1,0:T(8,128)(2,1)} fusion(bf16[512,12,64]{0,2,1:T(8,128)(2,1)S(1)} %bitcast.254, f32[12,512,1024]{2,1,0:T(8,128)} %get-tuple-element.137, f32[12,512]{1,0:T(8,128)S(1)} %log_add_fusion, pred[512,1024]{1,0:T(8,128)(4,1)S(1)} %copy-done.13), kind=kOutput, calls=%fused_computation.78 | convolution fusion | flops 831258624 | bytes 28073984 | tf_op jit(solution)/shard_map/hqk,qhe->khe/dot_general | solution.py:189
  603.2 8.2 fusion.13
  624.5 9.8 multiply_bitcast_fusion.1
  635.7 9.8 multiply_bitcast_fusion
  674.5 64.9 %reduce-scatter.31.cloned.1.call-done = bf16[48,1536]{1,0:T(8,128)(2,1)} async-done(((bf16[768,1536]{1,0:T(8,128)(2,1)}), bf16[48,1536]{1,0:T(8,128)(2,1)}) %reduce-scatter.31.cloned.1.call-update) | async-done | bytes 147472 | tf_op jit(solution)/shard_map/reduce_scatter | solution.py:225
  741.1 41.0 %all-reduce.10 = (f32[768,2]{0,1:T(2,128)S(1)}, f32[768,2]{0,1:T(2,128)S(1)}) all-reduce(f32[768,2]{0,1:T(2,128)S(1)} %maximum_add_fusion, f32[768,2]{0,1:T(2,128)S(1)} %maximum_add_fusion.1), channel_id=10, replica_groups=mesh['dp'=16,'tensor'=2] {'dp','tensor'}, use_global_device_ids=true, to_apply=%region_40.41.clone | all-reduce | flops 3072 | bytes 24576
  783.4 99.1 %reduce-scatter.29.cloned.1.call-done = bf16[48,2,1536]{2,0,1:T(8,128)(2,1)} async-done(((bf16[768,2,1536]{2,0,1:T(8,128)(2,1)}), bf16[48,2,1536]{2,0,1:T(8,128)(2,1)}) %reduce-scatter.29.cloned.1.call-update) | async-done | bytes 294928 | tf_op jit(solution)/shard_map/reduce_scatter | solution.py:225
  893.4 92.8 %reduce-scatter.27.cloned.1.call-done = f32[24,768]{1,0:T(8,128)} async-done(((f32[768,768]{1,0:T(8,128)}), f32[24,768]{1,0:T(8,128)}) %reduce-scatter.27.cloned.1.call-update) | async-done | bytes 73744 | tf_op jit(solution)/shard_map/reduce_scatter | solution.py:222
  986.2 125.1 %reduce-scatter.25.cloned.1.call-done = f32[24,3,768]{2,0,1:T(8,128)} async-done(((f32[768,3,768]{2,0,1:T(8,128)}), f32[24,3,768]{2,0,1:T(8,128)}) %reduce-scatter.25.cloned.1.call-update) | async-done | bytes 221200 | tf_op jit(solution)/shard_map/reduce_scatter | solution.py:222
  (361 shorter events, 208.9 us)
Async XLA Ops:
  7.2 90.8 %all-gather.11.cloned.1.call-start = ((), (), s32[]{:S(2)}) async-start(), calls=%async_computation.10 | async-start | bytes 3649536 | tf_op jit(solution)/shard_map/all_gather | solution.py:77
  7.9 137.6 %all-gather.13.cloned.1.call-start = ((), (), s32[]{:S(2)}) async-start(), calls=%async_computation.11 | async-start | bytes 1216512 | tf_op jit(solution)/shard_map/all_gather | solution.py:78
  8.6 166.2 %all-gather.15.cloned.1.call-start = ((), (), s32[]{:S(2)}) async-start(), calls=%async_computation.12 | async-start | bytes 2359296 | tf_op jit(solution)/shard_map/all_gather | solution.py:129
  10.4 50.0 %copy-start.85 = (bf16[24,2]{0,1:T(2,128)(2,1)S(1)}, bf16[24,2]{0,1:T(2,128)(2,1)}, u32[]{:S(2)}) copy-start(bf16[24,2]{0,1:T(2,128)(2,1)} %param.14) | copy-start | bytes 292
  13.7 131.9 %copy-start.47 = (bf16[1,1024,768]{2,1,0:T(8,128)(2,1)}, bf16[1,1024,768]{2,1,0:T(8,128)(2,1)S(1)}, u32[]{:S(2)}) copy-start(bf16[1,1024,768]{2,1,0:T(8,128)(2,1)S(1)} %get-tuple-element.90) | copy-start | bytes 4718596
  17.0 115.0 %copy-start.10 = (pred[512,1024]{1,0:T(8,128)(4,1)}, pred[512,1024]{1,0:T(8,128)(4,1)S(1)}, u32[]{:S(2)}) copy-start(pred[512,1024]{1,0:T(8,128)(4,1)S(1)} %broadcast_compare_fusion.1) | copy-start | bytes 1572868
  132.0 13.5 %copy-start.73 = (f32[12,512]{1,0:T(8,128)}, f32[12,512]{1,0:T(8,128)S(1)}, u32[]{:S(2)}) copy-start(f32[12,512]{1,0:T(8,128)S(1)} %log_add_fusion.1) | copy-start | bytes 73732
  149.6 92.2 %all-gather.17.cloned.1.call-start = ((), (), s32[]{:S(2)}) async-start(), calls=%async_computation.13 | async-start | bytes 5013504 | tf_op jit(solution)/shard_map/all_gather | solution.py:85
  150.4 155.0 %all-gather.19.cloned.1.call-start = ((), (), s32[]{:S(2)}) async-start(), calls=%async_computation.14 | async-start | bytes 2506752 | tf_op jit(solution)/shard_map/all_gather | solution.py:86
  151.0 188.5 %reduce-scatter.13.cloned.1.call-start = ((), (), s32[]{:S(2)}) async-start(), calls=%async_computation.15 | async-start | bytes 2359296 | tf_op jit(solution)/shard_map/reduce_scatter | solution.py:134
  151.5 175.0 %copy-start.12 = (pred[512,1024]{1,0:T(8,128)(4,1)}, pred[512,1024]{1,0:T(8,128)(4,1)S(1)}, u32[]{:S(2)}) copy-start(pred[512,1024]{1,0:T(8,128)(4,1)S(1)} %broadcast_compare_fusion) | copy-start | bytes 1572868
  311.8 39.8 %all-gather.21.cloned.1.call-start = ((), (), s32[]{:S(2)}) async-start(), calls=%async_computation.16 | async-start | bytes 2359296 | tf_op jit(solution)/shard_map/all_gather | solution.py:129
  342.9 37.0 %reduce-scatter.15.cloned.1.call-start = ((), (), s32[]{:S(2)}) async-start(), calls=%async_computation.17 | async-start | bytes 2359296 | tf_op jit(solution)/shard_map/reduce_scatter | solution.py:134
  369.5 30.9 %all-gather.25.cloned.1.call-start = ((), (), s32[]{:S(2)}) async-start(), calls=%async_computation.21 | async-start | bytes 2359296 | tf_op jit(solution)/shard_map/all_gather | solution.py:147
  389.2 32.0 %all-gather.23.cloned.1.call-start = ((), (), s32[]{:S(2)}) async-start(), calls=%async_computation.18 | async-start | bytes 2359296 | tf_op jit(solution)/shard_map/all_gather | solution.py:147
  391.7 50.3 %reduce-scatter.21.cloned.1.call-start = ((), (), s32[]{:S(2)}) async-start(), calls=%async_computation.22 | async-start | bytes 4718592 | tf_op jit(solution)/shard_map/reduce_scatter | solution.py:158
  421.1 33.1 %reduce-scatter.17.cloned.1.call-start = ((), (), s32[]{:S(2)}) async-start(), calls=%async_computation.19 | async-start | bytes 4718592 | tf_op jit(solution)/shard_map/reduce_scatter | solution.py:158
  441.9 203.5 %reduce-scatter.19.cloned.1.call-start = ((), (), s32[]{:S(2)}) async-start(), calls=%async_computation.20 | async-start | bytes 4718592 | tf_op jit(solution)/shard_map/reduce_scatter | solution.py:192
  499.5 17.1 %copy-start.49 = (bf16[512,12,32]{0,2,1:T(8,128)(2,1)S(1)}, bf16[512,12,32]{0,2,1:T(8,128)(2,1)}, u32[]{:S(2)}) copy-start(bf16[512,12,32]{0,2,1:T(8,128)(2,1)} %copy-done.48) | copy-start | bytes 1179652
  499.5 17.1 %copy-start.51 = (bf16[512,12,32]{0,2,1:T(8,128)(2,1)S(1)}, bf16[512,12,32]{0,2,1:T(8,128)(2,1)}, u32[]{:S(2)}) copy-start(bf16[512,12,32]{0,2,1:T(8,128)(2,1)} %copy-done.50) | copy-start | bytes 1179652
  525.6 127.5 %reduce-scatter.23.cloned.1.call-start = ((), (), s32[]{:S(2)}) async-start(), calls=%async_computation.23 | async-start | bytes 4718592 | tf_op jit(solution)/shard_map/reduce_scatter | solution.py:192
  553.1 17.1 %copy-start.53 = (bf16[512,12,32]{0,2,1:T(8,128)(2,1)S(1)}, bf16[512,12,32]{0,2,1:T(8,128)(2,1)}, u32[]{:S(2)}) copy-start(bf16[512,12,32]{0,2,1:T(8,128)(2,1)} %copy-done.52) | copy-start | bytes 1179652
  553.1 17.1 %copy-start.55 = (bf16[512,12,32]{0,2,1:T(8,128)(2,1)S(1)}, bf16[512,12,32]{0,2,1:T(8,128)(2,1)}, u32[]{:S(2)}) copy-start(bf16[512,12,32]{0,2,1:T(8,128)(2,1)} %copy-done.54) | copy-start | bytes 1179652
  592.9 146.4 %reduce-scatter.31.cloned.1.call-start = ((), (), s32[]{:S(2)}) async-start(), calls=%async_computation.27 | async-start | bytes 2506752 | tf_op jit(solution)/shard_map/reduce_scatter | solution.py:225
  603.1 279.4 %reduce-scatter.29.cloned.1.call-start = ((), (), s32[]{:S(2)}) async-start(), calls=%async_computation.26 | async-start | bytes 5013504 | tf_op jit(solution)/shard_map/reduce_scatter | solution.py:225
  618.6 367.6 %reduce-scatter.27.cloned.1.call-start = ((), (), s32[]{:S(2)}) async-start(), calls=%async_computation.25 | async-start | bytes 2433024 | tf_op jit(solution)/shard_map/reduce_scatter | solution.py:222
  634.3 477.0 %reduce-scatter.25.cloned.1.call-start = ((), (), s32[]{:S(2)}) async-start(), calls=%async_computation.24 | async-start | bytes 7299072 | tf_op jit(solution)/shard_map/reduce_scatter | solution.py:222
  671.3 69.7 %copy-start.82 = (f32[768]{0:T(1024)S(1)}, f32[768]{0:T(1024)}, u32[]{:S(2)}) copy-start(f32[768]{0:T(1024)} %get-tuple-element.61) | copy-start | bytes 9220
  671.3 69.7 %copy-start.81 = (f32[768]{0:T(1024)S(1)}, f32[768]{0:T(1024)}, u32[]{:S(2)}) copy-start(f32[768]{0:T(1024)} %get-tuple-element.126) | copy-start | bytes 9220
  671.3 69.7 %copy-start.80 = (f32[768]{0:T(1024)S(1)}, f32[768]{0:T(1024)}, u32[]{:S(2)}) copy-start(f32[768]{0:T(1024)} %get-tuple-element.52) | copy-start | bytes 9220
  671.3 69.7 %copy-start.79 = (f32[768]{0:T(1024)S(1)}, f32[768]{0:T(1024)}, u32[]{:S(2)}) copy-start(f32[768]{0:T(1024)} %get-tuple-element.128) | copy-start | bytes 9220
  671.6 213.0 %copy-start.21 = (f32[512,768]{1,0:T(8,128)S(1)}, f32[512,768]{1,0:T(8,128)}, u32[]{:S(2)}) copy-start(f32[512,768]{1,0:T(8,128)} %copy-done.19) | copy-start | bytes 4718596
  (77 other events, 271.0 us)
Sparse Core Ops, SparseCore 0:
  10.9 62.8 all-gather.10
  76.7 52.7 all-gather.12
  149.7 7.2 all-gather.14
  160.1 81.6 all-gather.16
  244.5 60.9 all-gather.18
  311.9 7.8 reduce-scatter.12
  343.0 8.5 all-gather.20
  369.6 10.2 reduce-scatter.14
  389.3 10.9 all-gather.24
  401.7 10.9 all-gather.22
  421.2 12.0 reduce-scatter.20
  442.0 12.0 reduce-scatter.16
  525.7 12.0 reduce-scatter.18
  593.1 12.0 reduce-scatter.22
  610.5 128.8 reduce-scatter.30
  745.2 137.1 reduce-scatter.28
  888.2 97.9 reduce-scatter.26
  993.3 118.0 reduce-scatter.24
where the time goes:
time: 1120 us
  waiting for transfers between devices  538 us (48%)
  matrix products  264 us (24%)
  blocking collectives  121 us (11%)
  other arithmetic  112 us (10%)
  local copies, waits for them, and re-layouts  66 us (6%)
  between operations  16 us (1%)
    reduce_scatter x2, waiting for transfers between devices, per_device(): lax.psum_scatter(attn_total, ('dp', 'tensor'), scatter_dimension=0, tiled...  218 us
    reduce_scatter x2, waiting for transfers between devices, per_device(): lax.psum_scatter(for_sending(mlp_total), 'dp', scatter_dimension=0, tiled...  164 us
    all_gather x1, waiting for transfers between devices, per_device(): lax.all_gather(gate_up, 'dp', axis=0, tiled=True)  67 us
    all_gather x1, waiting for transfers between devices, per_device(): lax.all_gather(down_weight, 'dp', axis=0, tiled=True)  48.7 us
    dot_general x2, matrix products, per_device(): jnp.einsum('qhe,khe->hqk', context_grad, values, preferred_element_type=j...  43.8 us
    all_gather x1, blocking collectives, per_device(): lax.all_gather(norm_gain, ('dp', 'tensor'), axis=0, tiled=True)  43.1 us
    unnamed x1, blocking collectives  41 us
    unnamed x184, local copies, waits for them, and re-layouts  39.8 us
  transfers between devices with their start and end apart: 18, of which 10 were waited for; matrix products, arithmetic and copies ran while one was open for 27% of the time, Pallas kernels for 0%

commit v1 on v0

--- a/solution.py
+++ b/solution.py
@@ -1,6 +1,8 @@
 import jax
 import jax.numpy as jnp
 from jax import lax
+from jax.experimental import pallas as pl
+from jax.experimental.pallas import tpu as pltpu
 from jax.sharding import PartitionSpec as P
 
 D = 768
@@ -66,7 +68,7 @@
     return tuple((left + right for left, right in zip(total, term)))
 
 
-def per_device(
+def general_device(
     tokens, segments, qkv_weight, out_weight, norm_gain, norm_shift, gate_up, down_weight, cotangent
 ):
     tensor_size = lax.axis_size("tensor")
@@ -236,6 +238,577 @@
     )
 
 
+HIDDEN = 1536
+WIDE = 3 * HIDDEN
+ATTN = 4 * D + 256
+PAIRS = HEADS // 2
+LANES = 2 * HEAD
+BLOCK = 256
+NBLOCK = SEQ // BLOCK
+ROWS = 256
+CHUNK = 512
+LOG2E = 1.4426950408889634
+F32 = jnp.float32
+BF16 = jnp.bfloat16
+
+
+def across(value, move):
+    pairs = []
+    for z in range(4):
+        for y in range(2):
+            for x in range(2):
+                for c in range(2):
+                    tz, ty, tx, tc = move(z, y, x, c)
+                    pairs.append((((z * 2 + y) * 2 + x) * 2 + c, ((tz * 2 + ty) * 2 + tx) * 2 + tc))
+    return lax.ppermute(value, ("dp", "tensor"), pairs)
+
+
+def core_swap(value):
+    return across(value, lambda z, y, x, c: (z, y, x, 1 - c))
+
+
+def first_swap(value):
+    return across(value, lambda z, y, x, c: (z, y, 1 - x, c) if c == 0 else (z, 1 - y, x, c))
+
+
+def second_swap(value):
+    return across(value, lambda z, y, x, c: (z, 1 - y, x, c) if c == 0 else (z, y, 1 - x, c))
+
+
+def depth_shift(value, steps):
+    return across(value, lambda z, y, x, c: ((z + steps) % 4, y, x, c))
+
+
+def slot_blocks(sign, core):
+    me = lax.axis_index("dp")
+    z, y, x = me // 4, (me // 2) % 2, me % 2
+    slot = jnp.arange(16, dtype=jnp.int32)
+    second, first, depth = slot // 8, (slot // 4) % 2, slot % 4
+    x_bit = jnp.where(core == 0, first, second)
+    y_bit = jnp.where(core == 0, second, first)
+    return (((z + sign * depth) % 4) * 4 + (y ^ y_bit) * 2 + (x ^ x_bit)).astype(jnp.int32)
+
+
+def gather_stages(block):
+    parts = [block] + [depth_shift(block, k) for k in (1, 2, 3)]
+    four = jnp.stack(parts, axis=0)
+    eight = jnp.concatenate([four, first_swap(four)], axis=0)
+    return eight, second_swap(eight)
+
+
+def reduce_stages(local):
+    once = local[0] + first_swap(local[1])
+    twice = once[0] + second_swap(once[1])
+    total = twice[0].astype(F32)
+    for k in (1, 2, 3):
+        total = total + depth_shift(twice[k], k).astype(F32)
+    return total
+
+
+def cost(flops, nbytes, trans=0):
+    return pl.CostEstimate(flops=int(flops), bytes_accessed=int(nbytes), transcendentals=int(trans))
+
+
+def params(vmem_mb, sem=("arbitrary",)):
+    return pltpu.CompilerParams(dimension_semantics=sem, vmem_limit_bytes=vmem_mb << 20)
+
+
+ANY = pl.BlockSpec(memory_space=pl.ANY)
+
+
+def assemble_attn(own, other, index):
+    def body(idx, a, b, c, d, out, sem):
+        copies = []
+        for i, ref in enumerate((a, b, c, d)):
+            for s in range(8):
+                copies.append(
+                    pltpu.make_async_copy(ref.at[s], out.at[idx[i * 8 + s]], sem.at[i * 8 + s])
+                )
+        for cp in copies:
+            cp.start()
+        for cp in copies:
+            cp.wait()
+
+    rows = own[0].shape[1]
+    return pl.pallas_call(
+        body,
+        grid_spec=pltpu.PrefetchScalarGridSpec(
+            num_scalar_prefetch=1,
+            grid=(1,),
+            in_specs=[ANY] * 4,
+            out_specs=ANY,
+            scratch_shapes=[pltpu.SemaphoreType.DMA((32,))],
+        ),
+        out_shape=jax.ShapeDtypeStruct((32, rows, ATTN), BF16),
+        compiler_params=params(16),
+        cost_estimate=cost(0, 4 * 32 * rows * ATTN),
+        name="assemble",
+    )(index, *own, *other)
+
+
+def turn(vector, cosine, sine):
+    lane = lax.broadcasted_iota(jnp.int32, vector.shape, 1)
+    swapped = jnp.where(
+        lane % HEAD < HEAD // 2,
+        pltpu.roll(vector, LANES - HEAD // 2, 1),
+        pltpu.roll(vector, HEAD // 2, 1),
+    )
+    return vector * cosine + swapped * sine
+
+
+def dot_nn(a, b):
+    return lax.dot_general(a, b, (((1,), (0,)), ((), ())), preferred_element_type=F32)
+
+
+def dot_nt(a, b):
+    return lax.dot_general(a, b, (((1,), (1,)), ((), ())), preferred_element_type=F32)
+
+
+def dot_tn(a, b):
+    return lax.dot_general(a, b, (((0,), (0,)), ((), ())), preferred_element_type=F32)
+
+
+def attn_forward(bounds, source, weights, cosine, sine, seg_col, seg_row):
+    def body(bnd, x, wq, wk, wv, cos, sin, sc, sr, q_out, k_out, v_out, ctx_out, lse_out):
+        low_lane = lax.broadcasted_iota(jnp.int32, (BLOCK, LANES), 1) < HEAD
+        for r in range(NBLOCK):
+            rows = pl.ds(r * BLOCK, BLOCK)
+            xr, cr, sn = x[rows, :], cos[rows, :], sin[rows, :]
+            q = turn(dot_nn(xr, wq[...]), cr, sn).astype(BF16)
+            q_out[rows, :] = q * jnp.asarray(HEAD**-0.5, BF16)
+            k_out[rows, :] = turn(dot_nn(xr, wk[...]), cr, sn).astype(BF16)
+            v_out[rows, :] = dot_nn(xr, wv[...]).astype(BF16)
+        for i in range(NBLOCK):
+            rows = pl.ds(i * BLOCK, BLOCK)
+            q = q_out[rows, :]
+            zero = jnp.zeros_like(q)
+            heads = (jnp.where(low_lane, q, zero), jnp.where(low_lane, zero, q))
+            own_seg = sc[rows, :]
+
+            def step(j, carry):
+                tops, sums, acc = carry
+                cols = pl.ds(pl.multiple_of(j * BLOCK, BLOCK), BLOCK)
+                k, v = k_out[cols, :], v_out[cols, :]
+                seen = own_seg == sr[:, cols]
+                new_tops, new_sums, alphas, parts = [], [], [], []
+                for h in range(2):
+                    s = jnp.where(seen, dot_nt(heads[h], k) * LOG2E, MASKED)
+                    top = jnp.maximum(tops[h], jnp.max(s, axis=1, keepdims=True))
+                    p = jnp.exp2(s - top)
+                    alpha = jnp.exp2(tops[h] - top)
+                    new_tops.append(top)
+                    alphas.append(alpha)
+                    new_sums.append(sums[h] * alpha + jnp.sum(p, axis=1, keepdims=True))
+                    parts.append(dot_nn(p.astype(BF16), v))
+                acc = acc * jnp.where(low_lane, alphas[0], alphas[1]) + jnp.where(
+                    low_lane, parts[0], parts[1]
+                )
+                return tuple(new_tops), tuple(new_sums), acc
+
+            start = jnp.full((BLOCK, 1), MASKED, F32)
+            none = jnp.zeros((BLOCK, 1), F32)
+            tops, sums, acc = lax.fori_loop(
+                bnd[i],
+                bnd[NBLOCK + i],
+                step,
+                ((start, start), (none, none), jnp.zeros((BLOCK, LANES), F32)),
+            )
+            ctx_out[rows, :] = (acc / jnp.where(low_lane, sums[0], sums[1])).astype(BF16)
+            both = jnp.where(
+                low_lane, tops[0] + jnp.log2(sums[0]), tops[1] + jnp.log2(sums[1])
+            )
+            flipped = both.T
+            lse_out[0, 0:1, i * BLOCK : (i + 1) * BLOCK] = flipped[0:1]
+            lse_out[0, 1:2, i * BLOCK : (i + 1) * BLOCK] = flipped[HEAD : HEAD + 1]
+
+    full = lambda shape: pl.BlockSpec(shape, lambda p, b: (0,) * len(shape))
+    column = lambda shift: pl.BlockSpec((D, LANES), lambda p, b: (0, shift * PAIRS + p))
+    pair = pl.BlockSpec((SEQ, LANES), lambda p, b: (0, p))
+    act = jax.ShapeDtypeStruct((SEQ, D), BF16)
+    return pl.pallas_call(
+        body,
+        grid_spec=pltpu.PrefetchScalarGridSpec(
+            num_scalar_prefetch=1,
+            grid=(PAIRS,),
+            in_specs=[
+                full((SEQ, D)),
+                column(0),
+                column(1),
+                column(2),
+                full((SEQ, LANES)),
+                full((SEQ, LANES)),
+                full((SEQ, 1)),
+                full((1, SEQ)),
+            ],
+            out_specs=[pair, pair, pair, pair, pl.BlockSpec((1, 8, SEQ), lambda p, b: (p, 0, 0))],
+        ),
+        out_shape=[act, act, act, act, jax.ShapeDtypeStruct((PAIRS, 8, SEQ), F32)],
+        compiler_params=params(32),
+        cost_estimate=cost(2 * SEQ * D * 3 * D + 16 * SEQ * SEQ * D, 16 << 20, HEADS * SEQ * SEQ),
+        name="attn_forward",
+    )(bounds, source, weights, weights, weights, cosine, sine, seg_col, seg_row)
+
+
+def attn_backward(bounds, q, k, v, ctx, ctx_grad, lse, cosine, sine, seg_col, seg_row):
+    def body(bnd, q, k, v, o, do, lse, cos, sin, sc, sr, out, qm, km, vm, dom, dq, dk, dv, dl):
+        low_lane = lax.broadcasted_iota(jnp.int32, (SEQ, LANES), 1) < HEAD
+        zero = jnp.zeros((SEQ, LANES), BF16)
+        for ref, kept in ((q, qm), (k, km), (v, vm), (do, dom)):
+            kept[0] = jnp.where(low_lane, ref[...], zero)
+            kept[1] = jnp.where(low_lane, zero, ref[...])
+        row = lax.broadcasted_iota(jnp.int32, (8, LANES), 0)
+        lane = lax.broadcasted_iota(jnp.int32, (8, LANES), 1)
+        pick = jnp.where(row == lane // HEAD, 1.0, 0.0).astype(F32)
+        product = do[...].astype(F32) * o[...].astype(F32)
+        dl[...] = lax.dot_general(
+            pick,
+            product,
+            (((1,), (1,)), ((), ())),
+            preferred_element_type=F32,
+            precision=lax.Precision.HIGHEST,
+        )
+        dk[...] = jnp.zeros_like(dk)
+        dv[...] = jnp.zeros_like(dv)
+        for i in range(NBLOCK):
+            rows = pl.ds(i * BLOCK, BLOCK)
+            own_seg = sr[:, rows]
+            lses = [lse[0, h : h + 1, i * BLOCK : (i + 1) * BLOCK] for h in range(2)]
+            deltas = [dl[h : h + 1, i * BLOCK : (i + 1) * BLOCK] for h in range(2)]
+
+            def step(j, acc):
+                cols = pl.ds(pl.multiple_of(j * BLOCK, BLOCK), BLOCK)
+                seen = sc[cols, :] == own_seg
+                probs, grads = [], []
+                for h in range(2):
+                    s = dot_nt(km[h, cols, :], q[rows, :]) * LOG2E - lses[h]
+                    p = jnp.exp2(jnp.where(seen, s, MASKED))
+                    dp = dot_nt(vm[h, cols, :], do[rows, :])
+                    probs.append(p.astype(BF16))
+                    grads.append((p * (dp - deltas[h])).astype(BF16))
+                dv[cols, :] += dot_nn(probs[0], dom[0, rows, :]) + dot_nn(probs[1], dom[1, rows, :])
+                dk[cols, :] += dot_nn(grads[0], qm[0, rows, :]) + dot_nn(grads[1], qm[1, rows, :])
+                return acc + dot_tn(grads[0], km[0, cols, :]) + dot_tn(grads[1], km[1, cols, :])
+
+            dq[rows, :] = lax.fori_loop(
+                bnd[i], bnd[NBLOCK + i], step, jnp.zeros((BLOCK, LANES), F32)
+            )
+        for r in range(NBLOCK):
+            rows = pl.ds(r * BLOCK, BLOCK)
+            cr, sn = cos[rows, :], -sin[rows, :]
+            out[0, rows, :] = turn(dq[rows, :] * (HEAD**-0.5), cr, sn).astype(BF16)
+            out[1, rows, :] = turn(dk[rows, :], cr, sn).astype(BF16)
+            out[2, rows, :] = dv[rows, :].astype(BF16)
+
+    full = lambda shape: pl.BlockSpec(shape, lambda p, b: (0,) * len(shape))
+    pair = pl.BlockSpec((SEQ, LANES), lambda p, b: (0, p))
+    low2 = pltpu.VMEM((2, SEQ, LANES), BF16)
+    wide = pltpu.VMEM((SEQ, LANES), F32)
+    return pl.pallas_call(
+        body,
+        grid_spec=pltpu.PrefetchScalarGridSpec(
+            num_scalar_prefetch=1,
+            grid=(PAIRS,),
+            in_specs=[
+                pair,
+                pair,
+                pair,
+                pair,
+                pair,
+                pl.BlockSpec((1, 8, SEQ), lambda p, b: (p, 0, 0)),
+                full((SEQ, LANES)),
+                full((SEQ, LANES)),
+                full((SEQ, 1)),
+                full((1, SEQ)),
+            ],
+            out_specs=pl.BlockSpec((3, SEQ, LANES), lambda p, b: (0, 0, p)),
+            scratch_shapes=[low2, low2, low2, low2, wide, wide, wide, pltpu.VMEM((8, SEQ), F32)],
+        ),
+        out_shape=jax.ShapeDtypeStruct((3, SEQ, D), BF16),
+        compiler_params=params(32),
+        cost_estimate=cost(40 * SEQ * SEQ * D, 16 << 20, HEADS * SEQ * SEQ),
+        name="attn_backward",
+    )(bounds, q, k, v, ctx, ctx_grad, lse, cosine, sine, seg_col, seg_row)
+
+
+def middle(index, source, ctx, cot, out_weight, norms, own, other):
+    def norm(v):
+        center = v - jnp.mean(v, axis=1, keepdims=True)
+        scale = lax.rsqrt(jnp.mean(center * center, axis=1, keepdims=True) + EPSILON)
+        return center * scale, scale
+
+    def norm_back(u, hat, scale, gain):
+        g = u * gain
+        return scale * (
+            g - jnp.mean(g, axis=1, keepdims=True) - hat * jnp.mean(g * hat, axis=1, keepdims=True)
+        )
+
+    def body(
+        idx, x, ctx, cot, wo, nrm, a, b, c, d,
+        out, normed_out, mlp_out, att_out, ctxg_out, hid_out, gu0, gu1, sw0, sw1, sums,
+        w, gate_s, up_s, sem,
+    ):
+        step = pl.program_id(0)
+
+        @pl.when(step == 0)
+        def _():
+            copies = []
+            for i, ref in enumerate((a, b, c, d)):
+                for s in range(8):
+                    n = i * 8 + s
+                    place = pl.ds(pl.multiple_of(idx[n] * 48, 16), 48)
+                    copies.append(
+                        pltpu.make_async_copy(ref.at[s], w.at[i // 2, place, :], sem.at[n])
+                    )
+            for cp in copies:
+                cp.start()
+            for cp in copies:
+                cp.wait()
+            sums[...] = jnp.zeros_like(sums)
+
+        gain1, gain2, shift1, shift2 = (nrm[i : i + 1, :] for i in range(4))
+        hidden_in = x[...].astype(F32) + dot_nn(ctx[...], wo[...])
+        hat1, scale1 = norm(hidden_in)
+        normed = hat1 * gain1 + shift1
+        low = normed.astype(BF16)
+        normed_out[...] = low
+        total = normed
+        for half in range(2):
+            sw = (sw0, sw1)[half]
+            for n in range(HIDDEN // CHUNK):
+                g_at, u_at, d_at = (pl.ds(p * HIDDEN + n * CHUNK, CHUNK) for p in range(3))
+                gate = dot_nn(low, w[half, :, g_at])
+                up = dot_nn(low, w[half, :, u_at])
+                gate_s[half, :, g_at] = gate
+                up_s[half, :, g_at] = up
+                act = (gate * jax.nn.sigmoid(gate) * up).astype(BF16)
+                sw[:, g_at] = act
+                total = total + dot_nt(act, w[half, :, d_at])
+        hat2, scale2 = norm(total)
+        out[...] = (hat2 * gain2 + shift2).astype(BF16)
+        u2 = cot[...].astype(F32)
+        resid = norm_back(u2, hat2, scale2, gain2)
+        mlp = resid.astype(BF16)
+        mlp_out[...] = mlp
+        back = resid
+        for half in range(2):
+            gu = (gu0, gu1)[half]
+            for n in range(HIDDEN // CHUNK):
+                g_at, u_at, d_at = (pl.ds(p * HIDDEN + n * CHUNK, CHUNK) for p in range(3))
+                grad = dot_nn(mlp, w[half, :, d_at])
+                gate, up = gate_s[half, :, g_at], up_s[half, :, g_at]
+                s = jax.nn.sigmoid(gate)
+                gate_grad = (grad * up * (s * (1.0 + gate * (1.0 - s)))).astype(BF16)
+                up_grad = (grad * (gate * s)).astype(BF16)
+                gu[:, g_at] = gate_grad
+                gu[:, u_at] = up_grad
+                back = back + dot_nt(gate_grad, w[half, :, g_at])
+                back = back + dot_nt(up_grad, w[half, :, u_at])
+        hidden_grad = norm_back(back, hat1, scale1, gain1)
+        hid_out[...] = hidden_grad
+        att = hidden_grad.astype(BF16)
+        att_out[...] = att
+        ctxg_out[...] = dot_nt(att, wo[...]).astype(BF16)
+        for i, v in enumerate((back * hat1, u2 * hat2, back, u2)):
+            sums[i : i + 1, :] += jnp.sum(v, axis=0, keepdims=True)
+
+    row = pl.BlockSpec((ROWS, D), lambda r, i: (r, 0))
+    wide = lambda n: pl.BlockSpec((ROWS, n), lambda r, i: (r, 0))
+    whole = lambda shape: pl.BlockSpec(shape, lambda r, i: (0,) * len(shape))
+    act = lambda n, t=BF16: jax.ShapeDtypeStruct((SEQ, n), t)
+    return pl.pallas_call(
+        body,
+        grid_spec=pltpu.PrefetchScalarGridSpec(
+            num_scalar_prefetch=1,
+            grid=(SEQ // ROWS,),
+            in_specs=[row, row, row, whole((D, D)), whole((8, D)), ANY, ANY, ANY, ANY],
+            out_specs=[row] * 6
+            + [wide(2 * HIDDEN)] * 2
+            + [wide(HIDDEN)] * 2
+            + [whole((8, D))],
+            scratch_shapes=[
+                pltpu.VMEM((2, D, WIDE), BF16),
+                pltpu.VMEM((2, ROWS, HIDDEN), F32),
+                pltpu.VMEM((2, ROWS, HIDDEN), F32),
+                pltpu.SemaphoreType.DMA((32,)),
+            ],
+        ),
+        out_shape=[
+            act(D),
+            act(D),
+            act(D),
+            act(D),
+            act(D),
+            act(D, F32),
+            act(2 * HIDDEN),
+            act(2 * HIDDEN),
+            act(HIDDEN),
+            act(HIDDEN),
+            jax.ShapeDtypeStruct((8, D), F32),
+        ],
+        compiler_params=params(56),
+        cost_estimate=cost(12 * SEQ * D * 2 * HIDDEN + 4 * SEQ * D * D, 60 << 20, 4 * SEQ * HIDDEN),
+        name="middle",
+    )(index, source, ctx, cot, out_weight, norms, *own, *other)
+
+
+def join_mlp(index, gu, gu_there, down, down_there):
+    def body(idx, a, b, c, d, out):
+        add = lambda p, q: (p[...].astype(F32) + q[...].astype(F32)).astype(BF16)
+        out[0, :, : 2 * HIDDEN] = add(a, b)
+        out[0, :, 2 * HIDDEN :] = add(c, d)
+
+    rows = D // 16
+    pick = lambda n: pl.BlockSpec((rows, n), lambda s, i: (i[s], 0))
+    return pl.pallas_call(
+        body,
+        grid_spec=pltpu.PrefetchScalarGridSpec(
+            num_scalar_prefetch=1,
+            grid=(16,),
+            in_specs=[pick(2 * HIDDEN), pick(2 * HIDDEN), pick(HIDDEN), pick(HIDDEN)],
+            out_specs=pl.BlockSpec((1, rows, WIDE), lambda s, i: (s, 0, 0)),
+        ),
+        out_shape=jax.ShapeDtypeStruct((16, rows, WIDE), BF16),
+        compiler_params=params(32),
+        cost_estimate=cost(D * WIDE, 6 * D * WIDE),
+        name="join_mlp",
+    )(index, gu, gu_there, down, down_there)
+
+
+def join_attn(index, grads, there):
+    def body(idx, a, b, out):
+        out[...] = (a[...].astype(F32) + b[...].astype(F32)).astype(BF16)
+
+    rows = D // 32
+    block = (1, rows, ATTN)
+    return pl.pallas_call(
+        body,
+        grid_spec=pltpu.PrefetchScalarGridSpec(
+            num_scalar_prefetch=1,
+            grid=(16,),
+            in_specs=[
+                pl.BlockSpec(block, lambda s, i: (i[s] * 2 + i[16], 0, 0)),
+                pl.BlockSpec(block, lambda s, i: (i[s], 0, 0)),
+            ],
+            out_specs=pl.BlockSpec(block, lambda s, i: (s, 0, 0)),
+        ),
+        out_shape=jax.ShapeDtypeStruct((16, rows, ATTN), BF16),
+        compiler_params=params(32),
+        cost_estimate=cost(D * ATTN // 2, 3 * D * ATTN),
+        name="join_attn",
+    )(index, grads, there)
+
+
+def rotary_lanes(segment_row):
+    labels = jnp.arange(NDOC + 1, dtype=jnp.int32)
+    before = jnp.sum((segment_row[None, :] < labels[:, None]).astype(jnp.int32), axis=1)
+    member = segment_row[:, None] == labels[None, :]
+    first = jnp.sum(jnp.where(member, before[None, :], 0), axis=1)
+    position = (jnp.arange(SEQ, dtype=jnp.int32) - first).astype(F32)
+    lane = jnp.arange(LANES) % (HEAD // 2)
+    frequency = jnp.power(F32(1000.0), -2.0 * lane.astype(F32) / HEAD)
+    angle = position[:, None] * frequency[None, :]
+    sign = jnp.where(jnp.arange(LANES) % HEAD < HEAD // 2, -1.0, 1.0)
+    ends = jnp.concatenate([before[1:], jnp.full((1,), SEQ, jnp.int32)])
+    heads = segment_row[::BLOCK]
+    tails = segment_row[BLOCK - 1 :: BLOCK]
+    low = jnp.sum(jnp.where(heads[:, None] == labels[None, :], before[None, :], 0), axis=1)
+    high = jnp.sum(jnp.where(tails[:, None] == labels[None, :], ends[None, :], 0), axis=1)
+    bounds = jnp.concatenate([low // BLOCK, (high + BLOCK - 1) // BLOCK]).astype(jnp.int32)
+    return jnp.cos(angle), jnp.sin(angle) * sign[None, :], bounds
+
+
+def sequence_device(
+    tokens, segments, qkv_weight, out_weight, norm_gain, norm_shift, gate_up, down_weight, cotangent
+):
+    core = lax.axis_index("tensor")
+    half = SEQ // 2
+
+    def ordered(mine, theirs):
+        return jnp.where(
+            core == 0, jnp.stack([mine, theirs], axis=0), jnp.stack([theirs, mine], axis=0)
+        )
+
+    pick = lambda a, i: lax.dynamic_index_in_dim(a, i, 0, keepdims=False)
+    source = pick(tokens, core)
+    segment_row = pick(segments, core)
+
+    attn_block = jnp.concatenate(
+        [
+            qkv_weight.reshape(-1, 3 * D),
+            out_weight,
+            norm_gain,
+            norm_shift,
+            jnp.zeros((out_weight.shape[0], 252), BF16),
+        ],
+        axis=1,
+    )
+    mlp_block = jnp.concatenate([gate_up.reshape(-1, 2 * HIDDEN), down_weight], axis=1)
+
+    from_here, from_there = slot_blocks(-1, core), slot_blocks(-1, 1 - core)
+    attn_own = gather_stages(attn_block)
+    attn_other = tuple(core_swap(part) for part in attn_own)
+    index = jnp.concatenate([from_here * 2 + core, from_there * 2 + 1 - core]).astype(jnp.int32)
+    weights = assemble_attn(attn_own, attn_other, index).reshape(D, ATTN)
+
+    mlp_own = gather_stages(mlp_block)
+    mlp_other = tuple(core_swap(part) for part in mlp_own)
+
+    cot = ordered(pick(cotangent, core), core_swap(pick(cotangent, 1 - core))).reshape(SEQ, D)
+    cosine, sine, bounds = rotary_lanes(segment_row)
+    seg_col, seg_row = segment_row[:, None], segment_row[None, :]
+
+    q, k, v, ctx, lse = attn_forward(bounds, source, weights, cosine, sine, seg_col, seg_row)
+    norms = weights[:, 4 * D : 4 * D + 8].astype(F32).T
+    norms = jnp.stack([norms[0], norms[1], norms[2], norms[3]] + [norms[4]] * 4, axis=0)
+    out_full = weights[:, 3 * D : 4 * D]
+    (out, normed, mlp_grad, att_grad, ctx_grad, hidden_grad, gu0, gu1, sw0, sw1, sums) = middle(
+        jnp.concatenate([from_here, from_there]), source, ctx, cot, out_full, norms, mlp_own, mlp_other
+    )
+
+    wgrad = lambda a, b: lax.dot_general(
+        a, b, (((0,), (0,)), ((), ())), preferred_element_type=F32
+    ).astype(BF16)
+    to_here = slot_blocks(1, core).reshape(2, 2, 4).transpose(1, 0, 2).reshape(16)
+    down_mine, down_theirs = wgrad(mlp_grad, sw0), wgrad(mlp_grad, sw1)
+    gu_mine, gu_theirs = wgrad(normed, gu0), wgrad(normed, gu1)
+    joined = join_mlp(to_here, gu_mine, core_swap(gu_theirs), down_mine, core_swap(down_theirs))
+    mlp_total = reduce_stages(joined.reshape(2, 2, 4, D // 16, WIDE))
+
+    projected = attn_backward(bounds, q, k, v, ctx, ctx_grad, lse, cosine, sine, seg_col, seg_row)
+    qkv_term = [wgrad(source, projected[i]) for i in range(3)]
+    out_term = wgrad(ctx, att_grad)
+    norm_term = jnp.pad(sums[:4].T, ((0, 0), (0, 252))).astype(BF16)
+    grads = jnp.concatenate(qkv_term + [out_term, norm_term], axis=1).reshape(16, 2, D // 32, ATTN)
+    leaving = lax.dynamic_index_in_dim(grads, 1 - core, 1, keepdims=False)
+    where = jnp.concatenate([to_here, core[None]]).astype(jnp.int32)
+    joined = join_attn(where, grads.reshape(32, D // 32, ATTN), core_swap(leaving))
+    attn_total = reduce_stages(joined.reshape(2, 2, 4, D // 32, ATTN))
+
+    input_grad = hidden_grad
+    for i in range(3):
+        input_grad = input_grad + lax.dot_general(
+            projected[i],
+            weights[:, i * D : (i + 1) * D],
+            (((1,), (1,)), ((), ())),
+            preferred_element_type=F32,
+        )
+
+    def spread(whole):
+        parts = whole.reshape(2, half, D)
+        return ordered(pick(parts, core), core_swap(pick(parts, 1 - core)))
+
+    return (
+        spread(out),
+        spread(input_grad),
+        attn_total[:, : 3 * D].reshape(-1, 3, D),
+        attn_total[:, 3 * D : 4 * D],
+        attn_total[:, 4 * D : 4 * D + 2],
+        attn_total[:, 4 * D + 2 : 4 * D + 4],
+        mlp_total[:, : 2 * HIDDEN].reshape(-1, 2, HIDDEN),
+        mlp_total[:, 2 * HIDDEN :],
+    )
+
+
 def solution(mesh):
     in_specs = (
         P("dp", None, None),
@@ -258,6 +831,13 @@
         P("dp", None, "tensor"),
         P("dp", "tensor"),
     )
+    sizes = dict(mesh.shape)
+
+    def per_device(tokens, *others):
+        if sizes["dp"] == 16 and sizes["tensor"] == 2 and tokens.shape[0] == 2:
+            return sequence_device(tokens, *others)
+        return general_device(tokens, *others)
+
     return jax.shard_map(
         per_device, mesh=mesh, in_specs=in_specs, out_specs=out_specs, check_vma=False
     )

time: 1120 us -> 564 us (0.50)
  waiting for transfers between devices: 538 us -> 194 us
  matrix products: 264 us -> 59 us
  Pallas kernels: 0 us -> 199 us
  blocking collectives: 121 us -> 0 us
  other arithmetic: 112 us -> 17.1 us
  starting transfers between devices: 1.35 us -> 32 us
  between operations: 16 us -> 1.4 us
    reduce_scatter x10 -> x0, waiting for transfers between devices: 403 us -> none  [the longest x2 218 us: per_device(): lax.psum_scatter(attn_total, ('dp', 'tensor'), scatter_dimension=0, tiled...]
    dot_general x38 -> x11, matrix products: 264 us -> 59 us  [the longest x8 46.8 us: sequence_device(): lax.dot_general(a, b, (((0,), (0,)), ((), ())), preferred_element_type=F32)]
    pallas_call x0 -> x6, Pallas kernels: none -> 199 us  [the longest x1 73.3 us: attn_forward(): pl.pallas_call(body, grid_spec=pltpu.PrefetchScalarGridSpec(num_scalar_pr...]
    ppermute x0 -> x30, waiting for transfers between devices: none -> 194 us  [across(): return lax.ppermute(value, ('dp', 'tensor'), pairs)]
    all_gather x8 -> x0, waiting for transfers between devices: 133 us -> none  [the longest x1 67 us: per_device(): lax.all_gather(gate_up, 'dp', axis=0, tiled=True)]
    all_gather x2 -> x0, blocking collectives: 79.8 us -> none  [the longest x1 43.1 us: per_device(): lax.all_gather(norm_gain, ('dp', 'tensor'), axis=0, tiled=True)]
    convert_element_type x10 -> x1, other arithmetic: 45.6 us -> 0.01 us  [rotary_lanes(): position = (jnp.arange(SEQ, dtype=jnp.int32) - first).astype(F32)]
    reduce_sum x17 -> x3, other arithmetic: 44.2 us -> 0.42 us  [the longest x1 0.21 us: rotary_lanes(): jnp.sum(jnp.where(tails[:, None] == labels[None, :], ends[None, :], 0), a...]
  transfers between devices with their start and end apart: 18 -> 30, of which waited for: 10 -> 13; matrix products, arithmetic and copies ran while one was open for 27% -> 19% of each run, Pallas kernels for 0% -> 25%
where the time goes in v1:
time: 564 us; the launch traced here: 562 us
  Pallas kernels  199 us (35%)
  waiting for transfers between devices  194 us (34%)
  local copies, waits for them, and re-layouts  60.1 us (11%)
  matrix products  59 us (10%)
  starting transfers between devices  32 us (6%)
  other arithmetic  17.1 us (3%)
    ppermute x30, waiting for transfers between devices, across(): return lax.ppermute(value, ('dp', 'tensor'), pairs)  194 us
    pallas_call x1, Pallas kernels, attn_forward(): pl.pallas_call(body, grid_spec=pltpu.PrefetchScalarGridSpec(num_scalar_pr...  73.3 us
    pallas_call x1, Pallas kernels, middle(): pl.pallas_call(body, grid_spec=pltpu.PrefetchScalarGridSpec(num_scalar_pr...  55.7 us
    pallas_call x1, Pallas kernels, attn_backward(): pl.pallas_call(body, grid_spec=pltpu.PrefetchScalarGridSpec(num_scalar_pr...  55 us
    dot_general x8, matrix products, sequence_device(): lax.dot_general(a, b, (((0,), (0,)), ((), ())), preferred_element_type=F32)  46.8 us
    ppermute x30, starting transfers between devices, across(): return lax.ppermute(value, ('dp', 'tensor'), pairs)  32 us
    unnamed x83, local copies, waits for them, and re-layouts  26.8 us
    dot_general x3, matrix products, sequence_device(): lax.dot_general(projected[i], weights[:, i * D:(i + 1) * D], (((1,), (1,)...  12.1 us
  transfers between devices with their start and end apart: 30, of which 13 were waited for; matrix products, arithmetic and copies ran while one was open for 19% of the time, Pallas kernels for 25%

profile of v1, /device:TPU:0, one launch (start us, length us, event | category | flops | bytes accessed | tf_op | source)
XLA Modules:
  0.0 562.0 jit_solution(13283404535365400589)
XLA Ops:
  4.1 5.1 collective-permute-start.2
  13.6 2.8 collective-permute-start.10
  20.1 2.6 constant_dynamic-slice_fusion.2
  26.1 5.2 collective-permute-done.10
  31.3 29.5 %collective-permute-done.9 = bf16[48,4608]{1,0:T(8,128)(2,1)} collective-permute-done((bf16[48,4608]{1,0:T(8,128)(2,1)}, bf16[48,4608]{1,0:T(8,128)(2,1)}, u32[]{:S(2)}, u32[]{:S(2)}) %collective-permute-start.9) | collective-permute-done | bytes 442400 | tf_op jit(solution)/shard_map/ppermute | solution.py:263
  68.4 16.5 %collective-permute-done.11 = bf16[4,48,4608]{2,1,0:T(8,128)(2,1)S(1)} collective-permute-done((bf16[4,48,4608]{2,1,0:T(8,128)(2,1)S(1)}, bf16[4,48,4608]{2,1,0:T(8,128)(2,1)S(1)}, u32[]{:S(2)}, u32[]{:S(2)}) %collective-permute-start.11) | collective-permute-done | bytes 1769504 | tf_op jit(solution)/shard_map/ppermute | solution.py:263
  93.9 34.2 %collective-permute-done.12.b = bf16[8,48,4608]{2,1,0:T(8,128)(2,1)} collective-permute-done((bf16[8,48,4608]{2,1,0:T(8,128)(2,1)}, bf16[8,48,4608]{2,1,0:T(8,128)(2,1)}, u32[]{:S(2)}, u32[]{:S(2)}) %collective-permute-start.12) | collective-permute-done | bytes 3538976 | tf_op jit(solution)/shard_map/ppermute | solution.py:263
  129.3 12.5 %collective-permute-done.4.b = bf16[8,24,3328]{2,1,0:T(8,128)(2,1)} collective-permute-done((bf16[8,24,3328]{2,1,0:T(8,128)(2,1)}, bf16[8,24,3328]{2,1,0:T(8,128)(2,1)}, u32[]{:S(2)}, u32[]{:S(2)}) %collective-permute-start.4) | collective-permute-done | bytes 1277984 | tf_op jit(solution)/shard_map/ppermute | solution.py:263
  144.3 3.0 fusion.14
  147.4 2.9 maximum_select_fusion.1
  150.3 3.4 assemble.1
  163.4 73.3 %attn_forward.1 = (bf16[1024,768]{1,0:T(8,128)(2,1)S(1)}, bf16[1024,768]{1,0:T(8,128)(2,1)S(1)}, bf16[1024,768]{1,0:T(8,128)(2,1)S(1)}, bf16[1024,768]{1,0:T(8,128)(2,1)S(1)}, f32[6,8,1024]{2,1,0:T(8,128)S(1)}) custom-call(s32[8]{0:T(128)S(1)} %pad_add_fusion.2.bnd, bf16[1024,768]{1,0:T(8,128)(2,1)S(1)} %copy-done.4, bf16[768,3328]{1,0:T(8,128)(2,1)S(1)} %bitcast.123, ...), custom_call_target="tpu_custom_call" | custom-call | flops 16508780544 | bytes 16777216 | tf_op jit(solution)/shard_map/attn_forward/pallas_call | solution.py:428
  237.9 55.7 %middle.1 = (bf16[1024,768]{1,0:T(8,128)(2,1)}, bf16[1024,768]{1,0:T(8,128)(2,1)}, bf16[1024,768]{1,0:T(8,128)(2,1)}, bf16[1024,768]{1,0:T(8,128)(2,1)}, bf16[10...) custom-call(s32[32]{0:T(128)} %pad_add_fusion.idx, ...), custom_call_target="tpu_custom_call" | custom-call | flops 31406948352 | bytes 62914560 | tf_op jit(solution)/shard_map/middle/pallas_call | solution.py:618
  293.6 6.6 %convolution_convert_fusion.2 = bf16[768,1536]{1,0:T(8,128)(2,1)} fusion(bf16[1024,768]{1,0:T(8,128)(2,1)} %get-tuple-element.37, bf16[1024,1536]{1,0:T(8,128)(2,1)} %get-tuple-element.39), kind=kOutput, calls=%fused_computation.2 | convolution fusion | flops 2417098752 | bytes 7077888 | tf_op jit(solution)/shard_map/dot_general | solution.py:768
  300.8 19.5 %convolution_convert_fusion = bf16[768,3072]{1,0:T(8,128)(2,1)} fusion(bf16[1024,768]{1,0:T(8,128)(2,1)S(1)} %copy-done.24, bf16[1024,3072]{1,0:T(8,128)(2,1)S(1)} %copy-done.22), kind=kOutput, calls=%fused_computation | convolution fusion | flops 4834197504 | bytes 12582912 | tf_op jit(solution)/shard_map/dot_general | solution.py:768
  320.3 55.0 %attn_backward.1 = bf16[3,1024,768]{2,1,0:T(8,128)(2,1)S(1)} custom-call(s32[8]{0:T(128)S(1)} %pad_add_fusion.2.bnd, bf16[1024,768]{1,0:T(8,128)(2,1)S(1)} %get-tuple-element.27.q, bf16[1024,768]{1,0:T(8,128)(2,1)S(1)} %get-tuple-element.28.k, bf16[1024,768]{1,0:T(8,128)(2,1)S(1)} %get-tuple-element.29.v, bf16[1024,768]{1,0:T(8,128)(2,1)S(1)} %copy-done.14, ...), custom_call_target="tpu_custom_call" | custom-call | flops 32212254720 | bytes 16777216 | tf_op jit(solution)/shard_map/attn_backward/pallas_call | solution.py:506
  386.8 7.8 %copy.60 = bf16[768,3328]{1,0:T(8,128)(2,1)} copy(bf16[768,3328]{0,1:T(8,128)(2,1)} %pad_dynamic-update-slice_fusion) | data formatting | bytes 10223616 | tf_op jit(solution)/shard_map/concatenate | solution.py:781
  394.6 3.5 dynamic-slice_bitcast_fusion
  398.7 5.1 convolution_convert_fusion.3.c
  403.9 3.1 fusion.6
  407.0 5.6 convolution_convert_fusion.1.a
  412.6 3.2 fusion.5
  415.8 9.9 %join_mlp.1 = bf16[16,48,4608]{2,1,0:T(8,128)(2,1)S(1)} custom-call(s32[16]{0:T(128)S(1)} %fusion.27.idx, bf16[768,3072]{1,0:T(8,128)(2,1)S(1)} %convolution_convert_fusion.1.a, bf16[768,3072]{1,0:T(8,128)(2,1)} %collective-permute-done.23.b, bf16[768,1536]{1,0:T(8,128)(2,1)S(1)} %convolution_convert_fusion.3.c, bf16[768,1536]{1,0:T(8,128)(2,1)} %collective-permute-done.24.d), custom_call_target="tpu_custom_call" | custom-call | flops 3538944 | bytes 21233664 | tf_op jit(solution)/shard_map/join_mlp/pallas_call | solution.py:662
  429.5 5.8 %add_add_fusion = f32[1024,768]{1,0:T(8,128)S(1)} fusion(f32[1024,768]{1,0:T(8,128)} %fusion.6, f32[1024,768]{1,0:T(8,128)} %get-tuple-element.26, f32[1024,768]{1,0:T(8,128)} %fusion.5, bf16[3,1024,768]{2,1,0:T(8,128)(2,1)} %copy-done.6, bf16[768,3328]{1,0:T(8,128)(2,1)S(1)} %bitcast.130), kind=kOutput, calls=%fused_computation.5 | convolution fusion | flops 1210318848 | bytes 15335424 | tf_op jit(solution)/shard_map/dot_general | solution.py:789
  444.8 38.6 %collective-permute-done.18 = bf16[2,4,24,3328]{3,2,1,0:T(8,128)(2,1)S(1)} collective-permute-done((bf16[2,4,24,3328]{3,2,1,0:T(8,128)(2,1)S(1)}, bf16[2,4,24,3328]{3,2,1,0:T(8,128)(2,1)S(1)}, u32[]{:S(2)}, u32[]{:S(2)}) %collective-permute-start.18) | collective-permute-done | bytes 1277984 | tf_op jit(solution)/shard_map/ppermute | solution.py:263
  487.0 7.2 %collective-permute-done.19 = bf16[4,24,3328]{2,1,0:T(8,128)(2,1)S(1)} collective-permute-done((bf16[4,24,3328]{2,1,0:T(8,128)(2,1)S(1)}, bf16[4,24,3328]{2,1,0:T(8,128)(2,1)S(1)}, u32[]{:S(2)}, u32[]{:S(2)}) %collective-permute-start.19) | collective-permute-done | bytes 639008 | tf_op jit(solution)/shard_map/ppermute | solution.py:263
  495.3 2.9 collective-permute-start.22
  499.1 14.1 %collective-permute-done.26 = bf16[4,48,4608]{2,1,0:T(8,128)(2,1)S(1)} collective-permute-done((bf16[4,48,4608]{2,1,0:T(8,128)(2,1)S(1)}, bf16[4,48,4608]{2,1,0:T(8,128)(2,1)S(1)}, u32[]{:S(2)}, u32[]{:S(2)}) %collective-permute-start.26) | collective-permute-done | bytes 1769504 | tf_op jit(solution)/shard_map/ppermute | solution.py:263
  515.7 2.9 collective-permute-start.29
  522.3 7.4 %collective-permute-done.27 = bf16[48,4608]{1,0:T(8,128)(2,1)S(1)} collective-permute-done((bf16[48,4608]{1,0:T(8,128)(2,1)S(1)}, bf16[48,4608]{1,0:T(8,128)(2,1)S(1)}, u32[]{:S(2)}, u32[]{:S(2)}) %collective-permute-start.27) | collective-permute-done | bytes 442400 | tf_op jit(solution)/shard_map/ppermute | solution.py:263
  529.7 6.6 %collective-permute-done.29 = bf16[48,4608]{1,0:T(8,128)(2,1)S(1)} collective-permute-done((bf16[48,4608]{1,0:T(8,128)(2,1)S(1)}, bf16[48,4608]{1,0:T(8,128)(2,1)S(1)}, u32[]{:S(2)}, u32[]{:S(2)}) %collective-permute-start.29) | collective-permute-done | bytes 442400 | tf_op jit(solution)/shard_map/ppermute | solution.py:263
  537.1 18.9 %collective-permute-done.28 = bf16[48,4608]{1,0:T(8,128)(2,1)} collective-permute-done((bf16[48,4608]{1,0:T(8,128)(2,1)S(1)}, bf16[48,4608]{1,0:T(8,128)(2,1)}, u32[]{:S(2)}, u32[]{:S(2)}) %collective-permute-start.28) | collective-permute-done | bytes 442400 | tf_op jit(solution)/shard_map/ppermute | solution.py:263
  (198 shorter events, 90.0 us)
Async XLA Ops:
  0.6 142.4 %copy-start = (bf16[2,1024,768]{2,1,0:T(8,128)(2,1)S(1)}, bf16[2,1024,768]{2,1,0:T(8,128)(2,1)}, u32[]{:S(2)}) copy-start(bf16[2,1024,768]{2,1,0:T(8,128)(2,1)} %param.9) | copy-start | bytes 9437188
  4.1 18.6 %collective-permute-start.2 = (bf16[24,3328]{1,0:T(8,128)(2,1)S(1)}, bf16[24,3328]{1,0:T(8,128)(2,1)S(1)}, u32[]{:S(2)}, u32[]{:S(2)}) collective-permute-start(bf16[24,3328]{1,0:T(8,128)(2,1)S(1)} %concatenate.36), channel_id=1, source_target_pairs={{0,24},{1,25},{2,26},{3,27},{4,28},{5,29},{6,30},{7,31},{8,0},{9,1... | collective-permute-start | bytes 479240 | tf_op jit(solution)/shard_map/ppermute | solution.py:263
  9.2 14.3 %collective-permute-start.1 = (bf16[24,3328]{1,0:T(8,128)(2,1)S(1)}, bf16[24,3328]{1,0:T(8,128)(2,1)}, u32[]{:S(2)}, u32[]{:S(2)}) collective-permute-start(bf16[24,3328]{1,0:T(8,128)(2,1)S(1)} %concatenate.36), channel_id=1, source_target_pairs={{0,16},{1,17},{2,18},{3,19},{4,20},{5,21},{6,22},{7,23},{8,24},{9,... | collective-permute-start | bytes 479240 | tf_op jit(solution)/shard_map/ppermute | solution.py:263
  9.2 14.3 %collective-permute-start = (bf16[24,3328]{1,0:T(8,128)(2,1)S(1)}, bf16[24,3328]{1,0:T(8,128)(2,1)}, u32[]{:S(2)}, u32[]{:S(2)}) collective-permute-start(bf16[24,3328]{1,0:T(8,128)(2,1)S(1)} %concatenate.36), channel_id=1, source_target_pairs={{0,8},{1,9},{2,10},{3,11},{4,12},{5,13},{6,14},{7,15},{8,16},{9,17... | collective-permute-start | bytes 479240 | tf_op jit(solution)/shard_map/ppermute | solution.py:263
  13.6 17.7 %collective-permute-start.10 = (bf16[48,4608]{1,0:T(8,128)(2,1)}, bf16[48,4608]{1,0:T(8,128)(2,1)}, u32[]{:S(2)}, u32[]{:S(2)}) collective-permute-start(bf16[48,4608]{1,0:T(8,128)(2,1)} %constant_dynamic-update-slice_fusion.5), channel_id=1, source_target_pairs={{0,24},{1,25},{2,26},{3,27},{4,28},{5,29},{6,30},{7,31},{8,0},{9,1... | collective-permute-start | bytes 1327112 | tf_op jit(solution)/shard_map/ppermute | solution.py:263
  16.4 44.5 %collective-permute-start.9 = (bf16[48,4608]{1,0:T(8,128)(2,1)}, bf16[48,4608]{1,0:T(8,128)(2,1)}, u32[]{:S(2)}, u32[]{:S(2)}) collective-permute-start(bf16[48,4608]{1,0:T(8,128)(2,1)} %constant_dynamic-update-slice_fusion.5), channel_id=1, source_target_pairs={{0,16},{1,17},{2,18},{3,19},{4,20},{5,21},{6,22},{7,23},{8,24},{9,... | collective-permute-start | bytes 1327112 | tf_op jit(solution)/shard_map/ppermute | solution.py:263
  22.8 38.1 %collective-permute-start.8 = (bf16[48,4608]{1,0:T(8,128)(2,1)}, bf16[48,4608]{1,0:T(8,128)(2,1)S(1)}, u32[]{:S(2)}, u32[]{:S(2)}) collective-permute-start(bf16[48,4608]{1,0:T(8,128)(2,1)} %constant_dynamic-update-slice_fusion.5), channel_id=1, source_target_pairs={{0,8},{1,9},{2,10},{3,11},{4,12},{5,13},{6,14},{7,15},{8,16},{9,17... | collective-permute-start | bytes 1327112 | tf_op jit(solution)/shard_map/ppermute | solution.py:263
  23.5 123.9 %collective-permute-start.7 = (bf16[512,768]{1,0:T(8,128)(2,1)}, bf16[512,768]{1,0:T(8,128)(2,1)}, u32[]{:S(2)}, u32[]{:S(2)}) collective-permute-start(bf16[512,768]{1,0:T(8,128)(2,1)} %get-tuple-element.88), channel_id=1, source_target_pairs={{0,1},{1,0},{2,3},{3,2},{4,5},{5,4},{6,7},{7,6},{8,9},{9,8},{10,11... | collective-permute-start | bytes 2359304 | tf_op jit(solution)/shard_map/ppermute | solution.py:263
  24.6 67.1 %collective-permute-start.3 = (bf16[4,24,3328]{2,1,0:T(8,128)(2,1)S(1)}, bf16[4,24,3328]{2,1,0:T(8,128)(2,1)S(1)}, u32[]{:S(2)}, u32[]{:S(2)}) collective-permute-start(bf16[4,24,3328]{2,1,0:T(8,128)(2,1)S(1)} %pad_maximum_fusion.1), channel_id=1, source_target_pairs={{0,2},{1,5},{2,0},{3,7},{4,6},{5,1},{6,4},{7,3},{8,10},{9,13},{10,... | collective-permute-start | bytes 1916936 | tf_op jit(solution)/shard_map/ppermute | solution.py:263
  62.3 22.6 %collective-permute-start.11 = (bf16[4,48,4608]{2,1,0:T(8,128)(2,1)S(1)}, bf16[4,48,4608]{2,1,0:T(8,128)(2,1)S(1)}, u32[]{:S(2)}, u32[]{:S(2)}) collective-permute-start(bf16[4,48,4608]{2,1,0:T(8,128)(2,1)S(1)} %pad_maximum_fusion), channel_id=1, source_target_pairs={{0,2},{1,5},{2,0},{3,7},{4,6},{5,1},{6,4},{7,3},{8,10},{9,13},{10,... | collective-permute-start | bytes 5308424 | tf_op jit(solution)/shard_map/ppermute | solution.py:263
  86.3 41.8 %collective-permute-start.12 = (bf16[8,48,4608]{2,1,0:T(8,128)(2,1)}, bf16[8,48,4608]{2,1,0:T(8,128)(2,1)}, u32[]{:S(2)}, u32[]{:S(2)}) collective-permute-start(bf16[8,48,4608]{2,1,0:T(8,128)(2,1)} %constant_dynamic-update-slice_fusion.7.a), channel_id=1, source_target_pairs={{0,4},{1,3},{2,6},{3,1},{4,0},{5,7},{6,2},{7,5},{8,12},{9,11},{10,... | collective-permute-start | bytes 10616840 | tf_op jit(solution)/shard_map/ppermute | solution.py:263
  92.5 49.2 %collective-permute-start.4 = (bf16[8,24,3328]{2,1,0:T(8,128)(2,1)}, bf16[8,24,3328]{2,1,0:T(8,128)(2,1)}, u32[]{:S(2)}, u32[]{:S(2)}) collective-permute-start(bf16[8,24,3328]{2,1,0:T(8,128)(2,1)} %constant_dynamic-update-slice_fusion.a), channel_id=1, source_target_pairs={{0,4},{1,3},{2,6},{3,1},{4,0},{5,7},{6,2},{7,5},{8,12},{9,11},{10,... | collective-permute-start | bytes 3833864 | tf_op jit(solution)/shard_map/ppermute | solution.py:263
  93.8 144.0 %collective-permute-start.13 = (bf16[8,48,4608]{2,1,0:T(8,128)(2,1)}, bf16[8,48,4608]{2,1,0:T(8,128)(2,1)}, u32[]{:S(2)}, u32[]{:S(2)}) collective-permute-start(bf16[8,48,4608]{2,1,0:T(8,128)(2,1)} %constant_dynamic-update-slice_fusion.7.a), channel_id=1, source_target_pairs={{0,1},{1,0},{2,3},{3,2},{4,5},{5,4},{6,7},{7,6},{8,9},{9,8},{10,11... | collective-permute-start | bytes 10616840 | tf_op jit(solution)/shard_map/ppermute | solution.py:263
  128.1 109.8 %collective-permute-start.14 = (bf16[8,48,4608]{2,1,0:T(8,128)(2,1)}, bf16[8,48,4608]{2,1,0:T(8,128)(2,1)}, u32[]{:S(2)}, u32[]{:S(2)}) collective-permute-start(bf16[8,48,4608]{2,1,0:T(8,128)(2,1)} %collective-permute-done.12.b), channel_id=1, source_target_pairs={{0,1},{1,0},{2,3},{3,2},{4,5},{5,4},{6,7},{7,6},{8,9},{9,8},{10,11... | collective-permute-start | bytes 10616840 | tf_op jit(solution)/shard_map/ppermute | solution.py:263
  128.7 21.6 %collective-permute-start.5 = (bf16[8,24,3328]{2,1,0:T(8,128)(2,1)}, bf16[8,24,3328]{2,1,0:T(8,128)(2,1)}, u32[]{:S(2)}, u32[]{:S(2)}) collective-permute-start(bf16[8,24,3328]{2,1,0:T(8,128)(2,1)} %constant_dynamic-update-slice_fusion.a), channel_id=1, source_target_pairs={{0,1},{1,0},{2,3},{3,2},{4,5},{5,4},{6,7},{7,6},{8,9},{9,8},{10,11... | collective-permute-start | bytes 3833864 | tf_op jit(solution)/shard_map/ppermute | solution.py:263
  141.8 8.5 %collective-permute-start.6 = (bf16[8,24,3328]{2,1,0:T(8,128)(2,1)}, bf16[8,24,3328]{2,1,0:T(8,128)(2,1)}, u32[]{:S(2)}, u32[]{:S(2)}) collective-permute-start(bf16[8,24,3328]{2,1,0:T(8,128)(2,1)} %collective-permute-done.4.b), channel_id=1, source_target_pairs={{0,1},{1,0},{2,3},{3,2},{4,5},{5,4},{6,7},{7,6},{8,9},{9,8},{10,11... | collective-permute-start | bytes 3833864 | tf_op jit(solution)/shard_map/ppermute | solution.py:263
  300.2 115.6 %collective-permute-start.24 = (bf16[768,1536]{1,0:T(8,128)(2,1)}, bf16[768,1536]{1,0:T(8,128)(2,1)}, u32[]{:S(2)}, u32[]{:S(2)}) collective-permute-start(bf16[768,1536]{1,0:T(8,128)(2,1)} %convolution_convert_fusion.2), channel_id=1, source_target_pairs={{0,1},{1,0},{2,3},{3,2},{4,5},{5,4},{6,7},{7,6},{8,9},{9,8},{10,11... | collective-permute-start | bytes 7077896 | tf_op jit(solution)/shard_map/ppermute | solution.py:263
  320.3 95.5 %collective-permute-start.23 = (bf16[768,3072]{1,0:T(8,128)(2,1)}, bf16[768,3072]{1,0:T(8,128)(2,1)}, u32[]{:S(2)}, u32[]{:S(2)}) collective-permute-start(bf16[768,3072]{1,0:T(8,128)(2,1)} %convolution_convert_fusion), channel_id=1, source_target_pairs={{0,1},{1,0},{2,3},{3,2},{4,5},{5,4},{6,7},{7,6},{8,9},{9,8},{10,11... | collective-permute-start | bytes 14155784 | tf_op jit(solution)/shard_map/ppermute | solution.py:263
  320.3 55.0 %copy-start.5 = (bf16[1024,768]{1,0:T(8,128)(2,1)S(1)}, bf16[1024,768]{1,0:T(8,128)(2,1)}, u32[]{:S(2)}) copy-start(bf16[1024,768]{1,0:T(8,128)(2,1)} %dynamic-slice_bitcast_fusion.2.x) | copy-start | bytes 4718596
  398.1 37.5 %collective-permute-start.17 = (bf16[16,24,3328]{2,1,0:T(8,128)(2,1)}, bf16[16,24,3328]{2,1,0:T(8,128)(2,1)S(1)}, u32[]{:S(2)}, u32[]{:S(2)}) collective-permute-start(bf16[16,24,3328]{2,1,0:T(8,128)(2,1)} %dynamic-slice_bitcast_fusion), channel_id=1, source_target_pairs={{0,1},{1,0},{2,3},{3,2},{4,5},{5,4},{6,7},{7,6},{8,9},{9,8},{10,11... | collective-permute-start | bytes 7667720 | tf_op jit(solution)/shard_map/ppermute | solution.py:263
  428.0 57.3 %collective-permute-start.25 = (bf16[2,4,48,4608]{3,2,1,0:T(8,128)(2,1)}, bf16[2,4,48,4608]{3,2,1,0:T(8,128)(2,1)S(1)}, u32[]{:S(2)}, u32[]{:S(2)}) collective-permute-start(bf16[2,4,48,4608]{3,2,1,0:T(8,128)(2,1)} %bitcast.140), channel_id=1, source_target_pairs={{0,2},{1,5},{2,0},{3,7},{4,6},{5,1},{6,4},{7,3},{8,10},{9,13},{10,... | collective-permute-start | bytes 10616840 | tf_op jit(solution)/shard_map/ppermute | solution.py:263
  435.6 7.3 %collective-permute-start.16 = (f32[512,768]{1,0:T(8,128)S(1)}, f32[512,768]{1,0:T(8,128)S(1)}, u32[]{:S(2)}, u32[]{:S(2)}) collective-permute-start(f32[512,768]{1,0:T(8,128)S(1)} %get-tuple-element.79), channel_id=1, source_target_pairs={{0,1},{1,0},{2,3},{3,2},{4,5},{5,4},{6,7},{7,6},{8,9},{9,8},{10,11... | collective-permute-start | bytes 4718600 | tf_op jit(solution)/shard_map/ppermute | solution.py:263
  437.3 46.1 %collective-permute-start.18 = (bf16[2,4,24,3328]{3,2,1,0:T(8,128)(2,1)S(1)}, bf16[2,4,24,3328]{3,2,1,0:T(8,128)(2,1)S(1)}, u32[]{:S(2)}, u32[]{:S(2)}) collective-permute-start(bf16[2,4,24,3328]{3,2,1,0:T(8,128)(2,1)S(1)} %bitcast.146), channel_id=1, source_target_pairs={{0,2},{1,5},{2,0},{3,7},{4,6},{5,1},{6,4},{7,3},{8,10},{9,13},{10,... | collective-permute-start | bytes 3833864 | tf_op jit(solution)/shard_map/ppermute | solution.py:263
  439.2 2.4 collective-permute-start.15
  483.8 10.5 %collective-permute-start.19 = (bf16[4,24,3328]{2,1,0:T(8,128)(2,1)S(1)}, bf16[4,24,3328]{2,1,0:T(8,128)(2,1)S(1)}, u32[]{:S(2)}, u32[]{:S(2)}) collective-permute-start(bf16[4,24,3328]{2,1,0:T(8,128)(2,1)S(1)} %slice_bitcast_fusion.13), channel_id=1, source_target_pairs={{0,4},{1,3},{2,6},{3,1},{4,0},{5,7},{6,2},{7,5},{8,12},{9,11},{10,... | collective-permute-start | bytes 1916936 | tf_op jit(solution)/shard_map/ppermute | solution.py:263
  486.4 26.8 %collective-permute-start.26 = (bf16[4,48,4608]{2,1,0:T(8,128)(2,1)S(1)}, bf16[4,48,4608]{2,1,0:T(8,128)(2,1)S(1)}, u32[]{:S(2)}, u32[]{:S(2)}) collective-permute-start(bf16[4,48,4608]{2,1,0:T(8,128)(2,1)S(1)} %slice_bitcast_fusion), channel_id=1, source_target_pairs={{0,4},{1,3},{2,6},{3,1},{4,0},{5,7},{6,2},{7,5},{8,12},{9,11},{10,... | collective-permute-start | bytes 5308424 | tf_op jit(solution)/shard_map/ppermute | solution.py:263
  494.4 24.3 %collective-permute-start.20 = (bf16[24,3328]{1,0:T(8,128)(2,1)S(1)}, bf16[24,3328]{1,0:T(8,128)(2,1)S(1)}, u32[]{:S(2)}, u32[]{:S(2)}) collective-permute-start(bf16[24,3328]{1,0:T(8,128)(2,1)S(1)} %get-tuple-element.89), channel_id=1, source_target_pairs={{0,8},{1,9},{2,10},{3,11},{4,12},{5,13},{6,14},{7,15},{8,16},{9,17... | collective-permute-start | bytes 479240 | tf_op jit(solution)/shard_map/ppermute | solution.py:263
  495.3 24.2 %collective-permute-start.22 = (bf16[24,3328]{1,0:T(8,128)(2,1)S(1)}, bf16[24,3328]{1,0:T(8,128)(2,1)S(1)}, u32[]{:S(2)}, u32[]{:S(2)}) collective-permute-start(bf16[24,3328]{1,0:T(8,128)(2,1)S(1)} %get-tuple-element.90), channel_id=1, source_target_pairs={{0,24},{1,25},{2,26},{3,27},{4,28},{5,29},{6,30},{7,31},{8,0},{9,1... | collective-permute-start | bytes 479240 | tf_op jit(solution)/shard_map/ppermute | solution.py:263
  498.2 21.3 %collective-permute-start.21 = (bf16[24,3328]{1,0:T(8,128)(2,1)S(1)}, bf16[24,3328]{1,0:T(8,128)(2,1)S(1)}, u32[]{:S(2)}, u32[]{:S(2)}) collective-permute-start(bf16[24,3328]{1,0:T(8,128)(2,1)S(1)} %get-tuple-element.91), channel_id=1, source_target_pairs={{0,16},{1,17},{2,18},{3,19},{4,20},{5,21},{6,22},{7,23},{8,24},{9,... | collective-permute-start | bytes 479240 | tf_op jit(solution)/shard_map/ppermute | solution.py:263
  514.7 15.0 %collective-permute-start.27 = (bf16[48,4608]{1,0:T(8,128)(2,1)S(1)}, bf16[48,4608]{1,0:T(8,128)(2,1)S(1)}, u32[]{:S(2)}, u32[]{:S(2)}) collective-permute-start(bf16[48,4608]{1,0:T(8,128)(2,1)S(1)} %get-tuple-element.82), channel_id=1, source_target_pairs={{0,8},{1,9},{2,10},{3,11},{4,12},{5,13},{6,14},{7,15},{8,16},{9,17... | collective-permute-start | bytes 1327112 | tf_op jit(solution)/shard_map/ppermute | solution.py:263
  515.7 20.7 %collective-permute-start.29 = (bf16[48,4608]{1,0:T(8,128)(2,1)S(1)}, bf16[48,4608]{1,0:T(8,128)(2,1)S(1)}, u32[]{:S(2)}, u32[]{:S(2)}) collective-permute-start(bf16[48,4608]{1,0:T(8,128)(2,1)S(1)} %get-tuple-element.83), channel_id=1, source_target_pairs={{0,24},{1,25},{2,26},{3,27},{4,28},{5,29},{6,30},{7,31},{8,0},{9,1... | collective-permute-start | bytes 1327112 | tf_op jit(solution)/shard_map/ppermute | solution.py:263
  518.6 37.4 %collective-permute-start.28 = (bf16[48,4608]{1,0:T(8,128)(2,1)S(1)}, bf16[48,4608]{1,0:T(8,128)(2,1)}, u32[]{:S(2)}, u32[]{:S(2)}) collective-permute-start(bf16[48,4608]{1,0:T(8,128)(2,1)S(1)} %get-tuple-element.84), channel_id=1, source_target_pairs={{0,16},{1,17},{2,18},{3,19},{4,20},{5,21},{6,22},{7,23},{8,24},{9,... | collective-permute-start | bytes 1327112 | tf_op jit(solution)/shard_map/ppermute | solution.py:263
  (32 other events, 229.4 us)
